TPU v7x, 32 devices: a whole 2x2x4 slice. The times are simulated.
32 devices in a mesh: ctx: 8 (over z, y), head: 4 (over x, core).
Axes of the slice: x: 2, y: 2, z: 4, core: 2. Of those that a mesh axis runs over, the one named last changes fastest.
Arguments:
- query_act: bfloat16 [2048, 2048], P('ctx', 'head'), may hold values from -5 to 5
- key_act: bfloat16 [2048, 2048], P('ctx', 'head'), may hold values from -5 to 5
- value_act: bfloat16 [2048, 2048], P('ctx', 'head'), may hold values from -6 to 6
- out_weight: bfloat16 [2048, 2048], P('head'), may hold values from -0.125 to 0.125
- cotangent: bfloat16 [2048, 2048], P('ctx', 'head'), may hold values from -6 to 6
- butterfly_cols: int32 [16, 3], replicated, may hold values from 0 to 15, as said below
- global_cols: int32 [256], replicated, may hold values from 0 to 2047, as said below
Outputs:
- layer_out: bfloat16 [2048, 2048], P('ctx', 'head')
- query_grad: bfloat16 [2048, 2048], P('ctx', 'head')
- key_grad: bfloat16 [2048, 2048], P('ctx', 'head')
- value_grad: bfloat16 [2048, 2048], P('ctx', 'head')
Inputs may be any that keep to these rules, and one draw needn't show every extreme that they name: `butterfly_cols`: entry [i, l] names one of the 2 blocks with index in the group (i // 2) xor 2**l, groups being runs of 2 consecutive block indices. `global_cols`: the positions are distinct.
All inputs are finite; a program needn't handle non-finite values.
Results may differ from a plain program's by a relative error of at most 0.0068.
Values may be sent and summed in bfloat16 or wider, within the bound.
No kernel may reach another device: no remote copies, remote signals or barrier semaphores. Data moves between devices by JAX's collectives and lax.ppermute only.
A program may use at most 64 MiB of HBM per device.

v0:
```python
import functools
import math

import jax
import jax.numpy as jnp
from jax import lax
from jax.experimental import pallas as pl
from jax.experimental.pallas import tpu as pltpu
from jax.sharding import PartitionSpec as P


HEAD_SIZE = 128
BLOCK = 128
STAT_ROWS = 8


FACTOR = 1.0 / math.sqrt(HEAD_SIZE)
NT = (((1,), (1,)), ((), ()))
TN = (((0,), (0,)), ((), ()))
F32 = jnp.float32
BF16 = jnp.bfloat16


def swap(shard, axis, mask):
    return lax.ppermute(shard, axis, [(i, i ^ mask) for i in range(lax.axis_size(axis))])


def call(kernel, out_shape, *operands, scalars=0, scratch=()):
    in_specs = [pl.BlockSpec(memory_space=pltpu.SMEM)] * scalars
    in_specs += [pl.BlockSpec(memory_space=pltpu.VMEM)] * (len(operands) - scalars)
    outs = jax.tree.map(lambda _: pl.BlockSpec(memory_space=pltpu.VMEM), out_shape)
    return pl.pallas_call(
        kernel, in_specs=in_specs, out_specs=outs, out_shape=out_shape, scratch_shapes=scratch
    )(*operands)


def like(shape, dtype=jnp.bfloat16):
    return jax.ShapeDtypeStruct(shape, dtype)


def dot(a, b, dims=(((1,), (0,)), ((), ()))):
    return lax.dot_general(a, b, dims, preferred_element_type=F32)


def block_at(index):
    return pl.ds(pl.multiple_of(index * BLOCK, BLOCK), BLOCK)


def columns_of(head):
    return pl.ds(pl.multiple_of(head * HEAD_SIZE, HEAD_SIZE), HEAD_SIZE)


def grad_kernel(weight_ref, *refs):
    pieces, out_ref = refs[:-1], refs[-1]
    width = pieces[0].shape[1]
    mine = lax.axis_index("head")
    total = None
    for m, piece in enumerate(pieces):
        start = pl.multiple_of(jnp.bitwise_xor(mine, m) * width, width)
        part = dot(piece[...], weight_ref[:, pl.ds(start, width)], NT)
        total = part if total is None else total + part
    out_ref[...] = total.astype(BF16)


def project_kernel(att_ref, weight_ref, *outs):
    width = outs[0].shape[1]
    mine = lax.axis_index("head")
    for m, out in enumerate(outs):
        start = pl.multiple_of(jnp.bitwise_xor(mine, m) * width, width)
        out[...] = dot(att_ref[...], weight_ref[:, pl.ds(start, width)]).astype(out.dtype)


def hot_kernel(masks, cols_ref, scatter_ref, *select_refs):
    rows, slots = scatter_ref.shape
    device = lax.axis_index("ctx")
    row_ids = lax.broadcasted_iota(jnp.int32, (rows, slots), 0)
    for mask, select_ref in zip(masks, select_refs):
        local = cols_ref[...] - jnp.bitwise_xor(device, mask) * rows
        chosen = (row_ids == local).astype(F32)
        if mask == 0:
            scatter_ref[...] = chosen.astype(BF16)
        select_ref[...] = chosen.T.astype(BF16)


def select_kernel(count, more, *refs):
    selects, keys, values = (refs[part * count : (part + 1) * count] for part in range(3))
    refs = refs[3 * count :]
    outs = refs[-2:]
    for sources, so_far, out in zip((keys, values), refs[:-2] if more else (None, None), outs):
        total = so_far[...].astype(F32) if more else 0.0
        for select, source in zip(selects, sources):
            total = total + dot(select[...], source[...])
        out[...] = total.astype(BF16)


def select_globals(selects, keys, values, so_far=()):
    shape = like((selects[0].shape[0], keys[0].shape[1]))
    kernel = functools.partial(select_kernel, len(selects), bool(so_far))
    return call(kernel, [shape, shape], *selects, *keys, *values, *so_far)


def query_kernel(strides, glob_parts, cols_ref, *refs):
    query, grad, own_key, own_value = refs[:4]
    refs = refs[4:]
    far_keys, far_values, refs = refs[:strides], refs[strides : 2 * strides], refs[2 * strides :]
    glob_keys, glob_values = refs[:glob_parts], refs[glob_parts : 2 * glob_parts]
    att_out, query_out, keep_out, send_out, stat_out, stats = refs[2 * glob_parts :]
    blocks = query.shape[0] // BLOCK
    heads = query.shape[1] // HEAD_SIZE
    near = (strides + 1) * BLOCK
    device = lax.axis_index("ctx")
    odd = jnp.bitwise_and(device, 1) == 1
    lane = lax.broadcasted_iota(jnp.int32, (BLOCK, BLOCK), 1)

    def one_head(head, _):
        part = columns_of(head)
        glob_key = sum((ref[:, part] for ref in glob_keys[1:]), glob_keys[0][:, part])
        glob_value = sum((ref[:, part] for ref in glob_values[1:]), glob_values[0][:, part])
        glob_grads, glob_weights = [], []
        for i in range(blocks):
            rows = pl.ds(i * BLOCK, BLOCK)
            picks = [
                block_at(
                    cols_ref[s, device * blocks + i] - jnp.bitwise_xor(device, 1 << s) * blocks
                )
                for s in range(strides)
            ]
            keys = jnp.concatenate(
                [own_key[rows, part]]
                + [far_keys[s][picks[s], part] for s in range(strides)]
                + [glob_key],
                0,
            )
            values = jnp.concatenate(
                [own_value[rows, part]]
                + [far_values[s][picks[s], part] for s in range(strides)]
                + [glob_value],
                0,
            )
            scores = dot(query[rows, part], keys, NT) * FACTOR
            top = jnp.max(scores, axis=1, keepdims=True)
            exponent = jnp.exp(scores - top)
            scale = 1.0 / jnp.sum(exponent, axis=1, keepdims=True)
            weights = exponent * scale
            rounded = weights.astype(BF16)
            att_out[rows, part] = dot(rounded, values).astype(BF16)
            prob_grad = dot(grad[rows, part], values, NT)
            delta = jnp.sum(weights * prob_grad, axis=1, keepdims=True)
            score_grad = (weights * (prob_grad - delta)).astype(BF16)
            query_out[rows, part] = (dot(score_grad, keys) * FACTOR).astype(BF16)
            glob_grads.append(score_grad[:, near:])
            glob_weights.append(rounded[:, near:])
            held = stats[rows, :]
            for place, column in enumerate((top, scale, delta)):
                held = jnp.where(lane == head * STAT_ROWS + place, column, held)
            stats[rows, :] = held
        key_term = dot(jnp.concatenate(glob_grads, 0), query[:, part], TN)
        value_term = dot(jnp.concatenate(glob_weights, 0), grad[:, part], TN)
        keep_out[:, part] = jnp.where(odd, value_term, key_term)
        send_out[:, part] = jnp.where(odd, key_term, value_term).astype(BF16)

    lax.fori_loop(0, heads, one_head, None)
    for i in range(blocks):
        rows = pl.ds(i * BLOCK, BLOCK)
        stat_out[:, rows] = stats[rows, :].T[: stat_out.shape[0]]


def query_side(cols, query, grad, key, value, far_keys, far_values, glob_keys, glob_values):
    rows, width = query.shape
    strides = len(far_keys)
    slots = glob_keys[0].shape[0]
    shapes = [
        like((rows, width)),
        like((rows, width)),
        like((slots, width), F32),
        like((slots, width)),
        like((width // HEAD_SIZE * STAT_ROWS, rows), F32),
    ]
    return call(
        functools.partial(query_kernel, strides, len(glob_keys)),
        shapes,
        cols,
        query,
        grad,
        key,
        value,
        *far_keys,
        *far_values,
        *glob_keys,
        *glob_values,
        scalars=1,
        scratch=[pltpu.VMEM((rows, BLOCK), F32)],
    )


def key_kernel(sources, cols_ref, key, value, *refs):
    count = len(sources)
    queries, grads, stats = (refs[part * count : (part + 1) * count] for part in range(3))
    so_far, (key_out, value_out) = refs[3 * count : -2], refs[-2:]
    blocks = key.shape[0] // BLOCK
    heads = key.shape[1] // HEAD_SIZE
    device = lax.axis_index("ctx")

    def one_head(head, _):
        part = columns_of(head)
        stat_at = pl.multiple_of(head * STAT_ROWS, STAT_ROWS)
        if so_far:
            key_out[:, part] = so_far[0][:, part]
            value_out[:, part] = so_far[1][:, part]
        for at, s in enumerate(sources):
            for i in range(blocks):
                rows = pl.ds(i * BLOCK, BLOCK)
                if s < 0:
                    place = rows
                else:
                    partner = jnp.bitwise_xor(device, 1 << s)
                    place = block_at(cols_ref[s, partner * blocks + i] - device * blocks)
                q, g = queries[at][rows, part], grads[at][rows, part]
                stat = stats[at][pl.ds(stat_at, STAT_ROWS), rows]
                top, scale, delta = stat[0:1], stat[1:2], stat[2:3]
                weights = jnp.exp(dot(key[place, part], q, NT) * FACTOR - top) * scale
                prob_grad = dot(value[place, part], g, NT)
                score_grad = (weights * (prob_grad - delta)).astype(BF16)
                key_term = dot(score_grad, q)
                value_term = dot(weights.astype(BF16), g)
                if s < 0:
                    key_out[place, part] = key_term
                    value_out[place, part] = value_term
                else:
                    key_out[place, part] += key_term
                    value_out[place, part] += value_term

    lax.fori_loop(0, heads, one_head, None)


def key_side(sources, cols, key, value, queries, grads, stats, so_far=()):
    shape = like(key.shape, F32)
    return call(
        functools.partial(key_kernel, sources),
        [shape, shape],
        cols,
        key,
        value,
        *queries,
        *grads,
        *stats,
        *so_far,
        scalars=1,
    )


def final_kernel(scatter, key, value, kept, got, key_out, value_out):
    odd = jnp.bitwise_and(lax.axis_index("ctx"), 1) == 1
    kept_rows = dot(scatter[...], kept[...])
    got_rows = dot(scatter[...], got[...])
    key_rows = jnp.where(odd, got_rows, kept_rows)
    value_rows = jnp.where(odd, kept_rows, got_rows)
    key_out[...] = ((key[...] + key_rows) * FACTOR).astype(BF16)
    value_out[...] = (value[...] + value_rows).astype(BF16)


def finish(scatter, key, value, kept, got):
    rows, width = key.shape
    slots = kept.shape[0]
    part = lambda count: pl.BlockSpec((count, width // 2), lambda h: (0, h))
    shape = like((rows, width))
    return pl.pallas_call(
        final_kernel,
        grid=(2,),
        in_specs=[pl.BlockSpec((rows, slots), lambda h: (0, 0))]
        + [part(rows)] * 2
        + [part(slots)] * 2,
        out_specs=[part(rows)] * 2,
        out_shape=[shape, shape],
        name="finish",
    )(scatter, key, value, kept, got)


def per_device(query_act, key_act, value_act, out_weight, cotangent, butterfly_cols, global_cols):
    strides = butterfly_cols.shape[1]
    groups = lax.axis_size("head")
    ring = strides == 3 and lax.axis_size("ctx") == 1 << strides
    cols = butterfly_cols.T
    slots = global_cols.shape[0]
    rows, width = key_act.shape
    masks = [1 << s for s in range(strides)]
    held = (0, 2, 6, 4) if ring else (0,)

    scatter, *selects = call(
        functools.partial(hot_kernel, held),
        [like((rows, slots))] + [like((slots, rows))] * len(held),
        global_cols.reshape(1, -1),
    )
    direct = (2, 6, 1) if ring else masks
    near = {m: (swap(key_act, "ctx", m), swap(value_act, "ctx", m)) for m in direct}
    pieces = [cotangent] + [swap(cotangent, "head", m) for m in range(1, groups)]
    near[0] = (key_act, value_act)
    if ring:
        near[4] = (swap(near[6][0], "ctx", 2), swap(near[2][1], "ctx", 6))
        first, last = held[:-1], held[-1]
        so_far = select_globals(
            selects[:-1], [near[m][0] for m in first], [near[m][1] for m in first]
        )
        glob_key, glob_value = select_globals(
            selects[-1:], [near[last][0]], [near[last][1]], so_far
        )
        glob_keys = [glob_key, swap(glob_key, "ctx", 1)]
        glob_values = [glob_value, swap(glob_value, "ctx", 1)]
    else:
        parts = select_globals(selects, [key_act], [value_act])
        glob_keys, glob_values = ([part] for part in lax.psum(tuple(parts), "ctx"))
    far_query = {m: swap(query_act, "ctx", m) for m in masks}
    attn_grad = call(grad_kernel, like((rows, width)), out_weight, *pieces)
    far_grad = {m: swap(attn_grad, "ctx", m) for m in masks}
    attention, query_grad, keep, send, stats = query_side(
        cols,
        query_act,
        attn_grad,
        key_act,
        value_act,
        [near[m][0] for m in masks],
        [near[m][1] for m in masks],
        glob_keys,
        glob_values,
    )
    far_stats = {m: swap(stats, "ctx", m) for m in masks}
    if ring:
        total = keep + swap(send, "ctx", 1).astype(F32)
        total = total + swap(total.astype(BF16), "ctx", 2).astype(F32)
        total = total + swap(total.astype(BF16), "ctx", 6).astype(F32)
        kept = total.astype(BF16)
        got = swap(kept, "ctx", 1)
    else:
        odd = jnp.bitwise_and(lax.axis_index("ctx"), 1) == 1
        send = send.astype(F32)
        key_term, value_term = lax.psum(
            (jnp.where(odd, send, keep), jnp.where(odd, keep, send)), "ctx"
        )
        kept = jnp.where(odd, value_term, key_term).astype(BF16)
        got = jnp.where(odd, key_term, value_term).astype(BF16)
    term = out_weight.shape[1] // groups
    shapes = [like((rows, term), F32 if m == 0 else BF16) for m in range(groups)]
    terms = call(project_kernel, shapes, attention, out_weight)
    layer_out = terms[0]
    for m in range(1, groups):
        layer_out = layer_out + swap(terms[m], "head", m).astype(F32)
    so_far = key_side((-1,), cols, key_act, value_act, [query_act], [attn_grad], [stats])
    key_sum, value_sum = key_side(
        tuple(range(strides)),
        cols,
        key_act,
        value_act,
        [far_query[m] for m in masks],
        [far_grad[m] for m in masks],
        [far_stats[m] for m in masks],
        so_far,
    )
    key_grad, value_grad = finish(scatter, key_sum, value_sum, kept, got)
    return (layer_out.astype(BF16), query_grad, key_grad, value_grad)


def solution(mesh):
    in_specs = (
        P("ctx", "head"),
        P("ctx", "head"),
        P("ctx", "head"),
        P("head", None),
        P("ctx", "head"),
        P(),
        P(),
    )
    out_specs = (P("ctx", "head"),) * 4

    return jax.shard_map(
        per_device, mesh=mesh, in_specs=in_specs, out_specs=out_specs, check_vma=False
    )
```

profile of v0, /device:TPU:0, one launch (start us, length us, event | category | flops | bytes accessed | tf_op | source)
XLA Modules:
  0.0 153.6 jit_solution(7454295301673862715)
XLA Ops:
  0.6 3.1 %collective-permute-start.8 = (bf16[256,512]{1,0:T(8,128)(2,1)}, bf16[256,512]{1,0:T(8,128)(2,1)S(1)}, u32[]{:S(2)}, u32[]{:S(2)}) collective-permute-start(bf16[256,512]{1,0:T(8,128)(2,1)} %value.3), channel_id=1, source_target_pairs={{0,8},{4,12},{8,0},{12,4},{16,24},{20,28},{24,16},{28,20},{1,9},{5... | collective-permute-start | bytes 786440 | tf_op jit(solution)/shard_map/ppermute | solution.py:25
  3.7 2.5 %collective-permute-start.5 = (bf16[256,512]{1,0:T(8,128)(2,1)}, bf16[256,512]{1,0:T(8,128)(2,1)S(1)}, u32[]{:S(2)}, u32[]{:S(2)}) collective-permute-start(bf16[256,512]{1,0:T(8,128)(2,1)} %key.3), channel_id=1, source_target_pairs={{0,24},{4,28},{8,16},{12,20},{16,8},{20,12},{24,0},{28,4},{1,25},{... | collective-permute-start | bytes 786440 | tf_op jit(solution)/shard_map/ppermute | solution.py:25
  6.2 0.7 collective-permute-start.4
  6.9 0.9 collective-permute-start.10
  7.8 3.3 %collective-permute-done.8.refs_7_.refs_8_ = bf16[256,512]{1,0:T(8,128)(2,1)S(1)} collective-permute-done((bf16[256,512]{1,0:T(8,128)(2,1)}, bf16[256,512]{1,0:T(8,128)(2,1)S(1)}, u32[]{:S(2)}, u32[]{:S(2)}) %collective-permute-start.8) | collective-permute-done | bytes 262176 | tf_op jit(solution)/shard_map/ppermute | solution.py:25
  11.1 9.7 %collective-permute-start.9 = (bf16[256,512]{1,0:T(8,128)(2,1)S(1)}, bf16[256,512]{1,0:T(8,128)(2,1)S(1)}, u32[]{:S(2)}, u32[]{:S(2)}) collective-permute-start(bf16[256,512]{1,0:T(8,128)(2,1)S(1)} %collective-permute-done.8.refs_7_.refs_8_), channel_id=1, source_target_pairs={{0,24},{4,28},{8,16},{12,20},{16,8},{20,12},{24,0},{28,4},{1,25},{... | collective-permute-start | bytes 786440 | tf_op jit(solution)/shard_map/ppermute | solution.py:25
  20.9 1.5 collective-permute-done.4.refs_4_.refs_5_
  22.4 2.1 %collective-permute-start.1 = (bf16[256,512]{1,0:T(8,128)(2,1)}, bf16[256,512]{1,0:T(8,128)(2,1)S(1)}, u32[]{:S(2)}, u32[]{:S(2)}) collective-permute-start(bf16[256,512]{1,0:T(8,128)(2,1)} %refs_0_.3), channel_id=1, source_target_pairs={{0,2},{1,3},{2,0},{3,1},{4,6},{5,7},{6,4},{7,5},{8,10},{9,11},{10,... | collective-permute-start | bytes 786440 | tf_op jit(solution)/shard_map/ppermute | solution.py:25
  24.5 1.6 %shard_map.103 = (bf16[256,256]{1,0:T(8,128)(2,1)}, bf16[256,256]{1,0:T(8,128)(2,1)}, bf16[256,256]{1,0:T(8,128)(2,1)}, bf16[256,256]{1,0:T(8,128)(2,1)}, bf16[256,256]{1,0:T(8,128)(2,1)}) custom-call(s32[1,256]{1,0:T(1,128)} %bitcast.5), custom_call_target="tpu_custom_call" | custom-call | tf_op jit(solution)/shard_map/pallas_call | solution.py:32
  26.1 4.5 %collective-permute-done.10.refs_8_ = bf16[256,512]{1,0:T(8,128)(2,1)S(1)} collective-permute-done((bf16[256,512]{1,0:T(8,128)(2,1)}, bf16[256,512]{1,0:T(8,128)(2,1)S(1)}, u32[]{:S(2)}, u32[]{:S(2)}) %collective-permute-start.10) | collective-permute-done | bytes 262176 | tf_op jit(solution)/shard_map/ppermute | solution.py:25
  31.3 2.8 %shard_map.104 = (bf16[256,512]{1,0:T(8,128)(2,1)}, bf16[256,512]{1,0:T(8,128)(2,1)}) custom-call(bf16[256,256]{1,0:T(8,128)(2,1)} %get-tuple-element.29.refs_0_, bf16[256,256]{1,0:T(8,128)(2,1)} %get-tuple-element.30.refs_1_, bf16[256,256]{1,0:T(8,128)(2,1)} %get-tuple-element.31.refs_2_, bf16[256,512]{1,0:T(8,128)(2,1)} %key.3, ...), custom_call_target="tpu_custom_call" | custom-call | tf_op jit(solution)/shard_map/pallas_call | solution.py:32
  34.1 2.1 %collective-permute-done.9.refs_2_.refs_9_ = bf16[256,512]{1,0:T(8,128)(2,1)S(1)} collective-permute-done((bf16[256,512]{1,0:T(8,128)(2,1)S(1)}, bf16[256,512]{1,0:T(8,128)(2,1)S(1)}, u32[]{:S(2)}, u32[]{:S(2)}) %collective-permute-start.9) | collective-permute-done | bytes 262176 | tf_op jit(solution)/shard_map/ppermute | solution.py:25
  36.2 1.5 collective-permute-start.3
  37.7 0.7 collective-permute-done.6.refs_1_.refs_6_
  38.4 1.7 %collective-permute-start.7 = (bf16[256,512]{1,0:T(8,128)(2,1)}, bf16[256,512]{1,0:T(8,128)(2,1)S(1)}, u32[]{:S(2)}, u32[]{:S(2)}) collective-permute-start(bf16[256,512]{1,0:T(8,128)(2,1)} %value.3), channel_id=1, source_target_pairs={{0,4},{4,0},{8,12},{12,8},{16,20},{20,16},{24,28},{28,24},{1,5},{5... | collective-permute-start | bytes 786440 | tf_op jit(solution)/shard_map/ppermute | solution.py:25
  40.0 2.3 %shard_map.105 = (bf16[256,512]{1,0:T(8,128)(2,1)}, bf16[256,512]{1,0:T(8,128)(2,1)}) custom-call(bf16[256,256]{1,0:T(8,128)(2,1)} %get-tuple-element.28.refs_0_, bf16[256,512]{1,0:T(8,128)(2,1)} %copy-done.6, bf16[256,512]{1,0:T(8,128)(2,1)} %copy-done.5, bf16[256,512]{1,0:T(8,128)(2,1)} %get-tuple-element.32.refs_3_, ...), custom_call_target="tpu_custom_call" | custom-call | tf_op jit(solution)/shard_map/pallas_call | solution.py:32
  42.3 0.7 collective-permute-start.11
  43.0 1.3 collective-permute-start.12
  44.4 0.7 copy-done.24
  45.1 3.3 %shard_map.102.refs_1_ = bf16[256,512]{1,0:T(8,128)(2,1)} custom-call(bf16[512,2048]{1,0:T(8,128)(2,1)} %weight_ref.3, bf16[256,512]{1,0:T(8,128)(2,1)} %refs_0_.3, bf16[256,512]{1,0:T(8,128)(2,1)} %copy-done.22, bf16[256,512]{1,0:T(8,128)(2,1)} %copy-done.23, bf16[256,512]{1,0:T(8,128)(2,1)} %copy-done.24), custom_call_target="tpu_custom_call" | custom-call | tf_op jit(solution)/shard_map/pallas_call | solution.py:32
  48.4 2.8 %collective-permute-done.7.refs_7_ = bf16[256,512]{1,0:T(8,128)(2,1)S(1)} collective-permute-done((bf16[256,512]{1,0:T(8,128)(2,1)}, bf16[256,512]{1,0:T(8,128)(2,1)S(1)}, u32[]{:S(2)}, u32[]{:S(2)}) %collective-permute-start.7) | collective-permute-done | bytes 262176 | tf_op jit(solution)/shard_map/ppermute | solution.py:25
  51.2 5.6 %collective-permute-done.11.refs_11_ = bf16[256,512]{1,0:T(8,128)(2,1)S(1)} collective-permute-done((bf16[256,512]{1,0:T(8,128)(2,1)}, bf16[256,512]{1,0:T(8,128)(2,1)S(1)}, u32[]{:S(2)}, u32[]{:S(2)}) %collective-permute-start.11) | collective-permute-done | bytes 262176 | tf_op jit(solution)/shard_map/ppermute | solution.py:25
  56.8 3.6 %collective-permute-done.12.refs_13_ = bf16[256,512]{1,0:T(8,128)(2,1)S(1)} collective-permute-done((bf16[256,512]{1,0:T(8,128)(2,1)}, bf16[256,512]{1,0:T(8,128)(2,1)S(1)}, u32[]{:S(2)}, u32[]{:S(2)}) %collective-permute-start.12) | collective-permute-done | bytes 262176 | tf_op jit(solution)/shard_map/ppermute | solution.py:25
  61.0 9.8 %shard_map.106 = (bf16[256,512]{1,0:T(8,128)(2,1)}, bf16[256,512]{1,0:T(8,128)(2,1)}, f32[256,512]{1,0:T(8,128)}, bf16[256,512]{1,0:T(8,128)(2,1)}, f32[32,256]{1,0:T(8,128)}) custom-call(s32[3,16]{1,0:T(4,128)} %bitcast.2, bf16[256,512]{1,0:T(8,128)(2,1)} %refs_0_.5, bf16[256,512]{1,0:T(8,128)(2,1)} %shard_map.102.refs_1_, bf16[256,512]{1,0:T(8,128)(2,1)} %key.3, ...), custom_call_target="tpu_custom_call" | custom-call | tf_op jit(solution)/shard_map/pallas_call | solution.py:32
  70.8 1.6 %collective-permute-start.25 = (bf16[256,512]{1,0:T(8,128)(2,1)}, bf16[256,512]{1,0:T(8,128)(2,1)S(1)}, u32[]{:S(2)}, u32[]{:S(2)}) collective-permute-start(bf16[256,512]{1,0:T(8,128)(2,1)} %get-tuple-element.49), channel_id=1, source_target_pairs={{0,4},{4,0},{8,12},{12,8},{16,20},{20,16},{24,28},{28,24},{1,5},{5... | collective-permute-start | bytes 786440 | tf_op jit(solution)/shard_map/ppermute | solution.py:25
  72.9 7.3 %collective-permute-done.25 = bf16[256,512]{1,0:T(8,128)(2,1)S(1)} collective-permute-done((bf16[256,512]{1,0:T(8,128)(2,1)}, bf16[256,512]{1,0:T(8,128)(2,1)S(1)}, u32[]{:S(2)}, u32[]{:S(2)}) %collective-permute-start.25) | collective-permute-done | bytes 262176 | tf_op jit(solution)/shard_map/ppermute | solution.py:25
  80.2 1.1 fusion
  81.3 6.3 %collective-permute-start.26 = (bf16[256,512]{1,0:T(8,128)(2,1)S(1)}, bf16[256,512]{1,0:T(8,128)(2,1)S(1)}, u32[]{:S(2)}, u32[]{:S(2)}) collective-permute-start(bf16[256,512]{1,0:T(8,128)(2,1)S(1)} %fusion), channel_id=1, source_target_pairs={{0,8},{4,12},{8,0},{12,4},{16,24},{20,28},{24,16},{28,20},{1,9},{5... | collective-permute-start | bytes 786440 | tf_op jit(solution)/shard_map/ppermute | solution.py:25
  87.7 3.6 %collective-permute-start.18 = (bf16[256,512]{1,0:T(8,128)(2,1)S(1)}, bf16[256,512]{1,0:T(8,128)(2,1)S(1)}, u32[]{:S(2)}, u32[]{:S(2)}) collective-permute-start(bf16[256,512]{1,0:T(8,128)(2,1)S(1)} %copy-done.4), channel_id=1, source_target_pairs={{0,16},{4,20},{8,24},{12,28},{16,0},{20,4},{24,8},{28,12},{1,17},{... | collective-permute-start | bytes 786440 | tf_op jit(solution)/shard_map/ppermute | solution.py:25
  91.3 1.5 collective-permute-start.19
  92.8 1.9 %collective-permute-start.20 = (bf16[256,512]{1,0:T(8,128)(2,1)S(1)}, bf16[256,512]{1,0:T(8,128)(2,1)S(1)}, u32[]{:S(2)}, u32[]{:S(2)}) collective-permute-start(bf16[256,512]{1,0:T(8,128)(2,1)S(1)} %copy-done.1), channel_id=1, source_target_pairs={{0,8},{4,12},{8,0},{12,4},{16,24},{20,28},{24,16},{28,20},{1,9},{5... | collective-permute-start | bytes 786440 | tf_op jit(solution)/shard_map/ppermute | solution.py:25
  94.8 7.7 %collective-permute-done.26 = bf16[256,512]{1,0:T(8,128)(2,1)S(1)} collective-permute-done((bf16[256,512]{1,0:T(8,128)(2,1)S(1)}, bf16[256,512]{1,0:T(8,128)(2,1)S(1)}, u32[]{:S(2)}, u32[]{:S(2)}) %collective-permute-start.26) | collective-permute-done | bytes 262176 | tf_op jit(solution)/shard_map/ppermute | solution.py:25
  102.5 1.8 %collective-permute-start.21 = (bf16[256,512]{1,0:T(8,128)(2,1)S(1)}, bf16[256,512]{1,0:T(8,128)(2,1)S(1)}, u32[]{:S(2)}, u32[]{:S(2)}) collective-permute-start(bf16[256,512]{1,0:T(8,128)(2,1)S(1)} %copy-done.1), channel_id=1, source_target_pairs={{0,16},{4,20},{8,24},{12,28},{16,0},{20,4},{24,8},{28,12},{1,17},{... | collective-permute-start | bytes 786440 | tf_op jit(solution)/shard_map/ppermute | solution.py:25
  104.2 1.1 fusion.1
  105.4 2.0 %collective-permute-done.17.refs_1_ = bf16[256,512]{1,0:T(8,128)(2,1)S(1)} collective-permute-done((bf16[256,512]{1,0:T(8,128)(2,1)S(1)}, bf16[256,512]{1,0:T(8,128)(2,1)S(1)}, u32[]{:S(2)}, u32[]{:S(2)}) %collective-permute-start.17) | collective-permute-done | bytes 262176 | tf_op jit(solution)/shard_map/ppermute | solution.py:25
  107.4 5.1 %collective-permute-start.27 = (bf16[256,512]{1,0:T(8,128)(2,1)S(1)}, bf16[256,512]{1,0:T(8,128)(2,1)S(1)}, u32[]{:S(2)}, u32[]{:S(2)}) collective-permute-start(bf16[256,512]{1,0:T(8,128)(2,1)S(1)} %fusion.1), channel_id=1, source_target_pairs={{0,24},{4,28},{8,16},{12,20},{16,8},{20,12},{24,0},{28,4},{1,25},{... | collective-permute-start | bytes 786440 | tf_op jit(solution)/shard_map/ppermute | solution.py:25
  112.5 1.7 %collective-permute-start.22 = (f32[32,256]{1,0:T(8,128)S(1)}, f32[32,256]{1,0:T(8,128)S(1)}, u32[]{:S(2)}, u32[]{:S(2)}) collective-permute-start(f32[32,256]{1,0:T(8,128)S(1)} %copy-done.28), channel_id=1, source_target_pairs={{0,4},{4,0},{8,12},{12,8},{16,20},{20,16},{24,28},{28,24},{1,5},{5... | collective-permute-start | bytes 98312 | tf_op jit(solution)/shard_map/ppermute | solution.py:25
  114.2 3.3 %collective-permute-start.24 = (f32[32,256]{1,0:T(8,128)S(1)}, f32[32,256]{1,0:T(8,128)S(1)}, u32[]{:S(2)}, u32[]{:S(2)}) collective-permute-start(f32[32,256]{1,0:T(8,128)S(1)} %copy-done.28), channel_id=1, source_target_pairs={{0,16},{4,20},{8,24},{12,28},{16,0},{20,4},{24,8},{28,12},{1,17},{... | collective-permute-start | bytes 98312 | tf_op jit(solution)/shard_map/ppermute | solution.py:25
  117.5 4.1 %shard_map.108 = (f32[256,512]{1,0:T(8,128)}, f32[256,512]{1,0:T(8,128)}) custom-call(s32[3,16]{1,0:T(4,128)} %bitcast.3, bf16[256,512]{1,0:T(8,128)(2,1)} %key.3, bf16[256,512]{1,0:T(8,128)(2,1)} %value.3, bf16[256,512]{1,0:T(8,128)(2,1)} %refs_0_.5, bf16[256,512]{1,0:T(8,128)(2,1)} %shard_map.102.refs_1_, f32[32,256]{1,0:T(8,128)} %get-tuple-element.43.refs_2_), custom_call_target="tpu_custom_call" | custom-call | tf_op jit(solution)/shard_map/pallas_call | solution.py:32
  121.7 3.1 %shard_map.107 = (f32[256,512]{1,0:T(8,128)}, bf16[256,512]{1,0:T(8,128)(2,1)}, bf16[256,512]{1,0:T(8,128)(2,1)}, bf16[256,512]{1,0:T(8,128)(2,1)}) custom-call(bf16[256,512]{1,0:T(8,128)(2,1)} %get-tuple-element.36.att_ref, bf16[512,2048]{1,0:T(8,128)(2,1)} %weight_ref.3), custom_call_target="tpu_custom_call" | custom-call | tf_op jit(solution)/shard_map/pallas_call | solution.py:32
  125.4 7.6 %collective-permute-start.14 = (bf16[256,512]{1,0:T(8,128)(2,1)}, bf16[256,512]{1,0:T(8,128)(2,1)S(1)}, u32[]{:S(2)}, u32[]{:S(2)}) collective-permute-start(bf16[256,512]{1,0:T(8,128)(2,1)} %get-tuple-element.39), channel_id=1, source_target_pairs={{0,2},{1,3},{2,0},{3,1},{4,6},{5,7},{6,4},{7,5},{8,10},{9,11},{10,... | collective-permute-start | bytes 786440 | tf_op jit(solution)/shard_map/ppermute | solution.py:25
  133.8 7.7 %shard_map.109 = (f32[256,512]{1,0:T(8,128)}, f32[256,512]{1,0:T(8,128)}) custom-call(s32[3,16]{1,0:T(4,128)} %bitcast.4, bf16[256,512]{1,0:T(8,128)(2,1)} %key.3, bf16[256,512]{1,0:T(8,128)(2,1)} %value.3, bf16[256,512]{1,0:T(8,128)(2,1)} %copy-done.16, bf16[256,512]{1,0:T(8,128)(2,1)} %copy-done.17, bf16[256,512]{1,0:T(8,128)(2,1)} %copy-done.18, ...), custom_call_target="tpu_custom_call" | custom-call | tf_op jit(solution)/shard_map/pallas_call | solution.py:32
  141.6 1.6 %collective-permute-start.28 = (bf16[256,512]{1,0:T(8,128)(2,1)S(1)}, bf16[256,512]{1,0:T(8,128)(2,1)S(1)}, u32[]{:S(2)}, u32[]{:S(2)}) collective-permute-start(bf16[256,512]{1,0:T(8,128)(2,1)S(1)} %add_convert_fusion.kept), channel_id=1, source_target_pairs={{0,4},{4,0},{8,12},{12,8},{16,20},{20,16},{24,28},{28,24},{1,5},{5... | collective-permute-start | bytes 786440 | tf_op jit(solution)/shard_map/ppermute | solution.py:25
  143.2 2.3 %collective-permute-done.15 = bf16[256,512]{1,0:T(8,128)(2,1)S(1)} collective-permute-done((bf16[256,512]{1,0:T(8,128)(2,1)}, bf16[256,512]{1,0:T(8,128)(2,1)S(1)}, u32[]{:S(2)}, u32[]{:S(2)}) %collective-permute-start.15) | collective-permute-done | bytes 262176 | tf_op jit(solution)/shard_map/ppermute | solution.py:25
  145.6 0.8 add_convert_fusion.1
  146.4 4.0 %collective-permute-done.28.got = bf16[256,512]{1,0:T(8,128)(2,1)S(1)} collective-permute-done((bf16[256,512]{1,0:T(8,128)(2,1)S(1)}, bf16[256,512]{1,0:T(8,128)(2,1)S(1)}, u32[]{:S(2)}, u32[]{:S(2)}) %collective-permute-start.28) | collective-permute-done | bytes 262176 | tf_op jit(solution)/shard_map/ppermute | solution.py:25
  150.4 0.7 copy-done.15
  151.1 2.5 %finish.1 = (bf16[256,512]{1,0:T(8,128)(2,1)}, bf16[256,512]{1,0:T(8,128)(2,1)}) custom-call(bf16[256,256]{1,0:T(8,128)(2,1)} %get-tuple-element.42.scatter, f32[256,512]{1,0:T(8,128)} %get-tuple-element.46.key, f32[256,512]{1,0:T(8,128)} %get-tuple-element.47.value, bf16[256,512]{1,0:T(8,128)(2,1)} %copy-done.7, bf16[256,512]{1,0:T(8,128)(2,1)} %copy-done.15), custom_call_target="tpu_custom_call" | custom-call | tf_op jit(solution)/shard_map/finish/pallas_call | solution.py:267
  (81 shorter events, 3.6 us)
Async XLA Ops:
  0.6 10.5 %collective-permute-start.8 = (bf16[256,512]{1,0:T(8,128)(2,1)}, bf16[256,512]{1,0:T(8,128)(2,1)S(1)}, u32[]{:S(2)}, u32[]{:S(2)}) collective-permute-start(bf16[256,512]{1,0:T(8,128)(2,1)} %value.3), channel_id=1, source_target_pairs={{0,8},{4,12},{8,0},{12,4},{16,24},{20,28},{24,16},{28,20},{1,9},{5... | collective-permute-start | bytes 786440 | tf_op jit(solution)/shard_map/ppermute | solution.py:25
  3.7 17.0 %collective-permute-start.5 = (bf16[256,512]{1,0:T(8,128)(2,1)}, bf16[256,512]{1,0:T(8,128)(2,1)S(1)}, u32[]{:S(2)}, u32[]{:S(2)}) collective-permute-start(bf16[256,512]{1,0:T(8,128)(2,1)} %key.3), channel_id=1, source_target_pairs={{0,24},{4,28},{8,16},{12,20},{16,8},{20,12},{24,0},{28,4},{1,25},{... | collective-permute-start | bytes 786440 | tf_op jit(solution)/shard_map/ppermute | solution.py:25
  6.2 16.1 %collective-permute-start.4 = (bf16[256,512]{1,0:T(8,128)(2,1)}, bf16[256,512]{1,0:T(8,128)(2,1)S(1)}, u32[]{:S(2)}, u32[]{:S(2)}) collective-permute-start(bf16[256,512]{1,0:T(8,128)(2,1)} %key.3), channel_id=1, source_target_pairs={{0,8},{4,12},{8,0},{12,4},{16,24},{20,28},{24,16},{28,20},{1,9},{5... | collective-permute-start | bytes 786440 | tf_op jit(solution)/shard_map/ppermute | solution.py:25
  6.9 23.7 %collective-permute-start.10 = (bf16[256,512]{1,0:T(8,128)(2,1)}, bf16[256,512]{1,0:T(8,128)(2,1)S(1)}, u32[]{:S(2)}, u32[]{:S(2)}) collective-permute-start(bf16[256,512]{1,0:T(8,128)(2,1)} %value.3), channel_id=1, source_target_pairs={{0,24},{4,28},{8,16},{12,20},{16,8},{20,12},{24,0},{28,4},{1,25},{... | collective-permute-start | bytes 786440 | tf_op jit(solution)/shard_map/ppermute | solution.py:25
  11.1 19.5 %copy-start.2 = (bf16[256,512]{1,0:T(8,128)(2,1)}, bf16[256,512]{1,0:T(8,128)(2,1)S(1)}, u32[]{:S(2)}) copy-start(bf16[256,512]{1,0:T(8,128)(2,1)S(1)} %collective-permute-done.8.refs_7_.refs_8_) | copy-start | bytes 786436
  11.1 25.0 %collective-permute-start.9 = (bf16[256,512]{1,0:T(8,128)(2,1)S(1)}, bf16[256,512]{1,0:T(8,128)(2,1)S(1)}, u32[]{:S(2)}, u32[]{:S(2)}) collective-permute-start(bf16[256,512]{1,0:T(8,128)(2,1)S(1)} %collective-permute-done.8.refs_7_.refs_8_), channel_id=1, source_target_pairs={{0,24},{4,28},{8,16},{12,20},{16,8},{20,12},{24,0},{28,4},{1,25},{... | collective-permute-start | bytes 786440 | tf_op jit(solution)/shard_map/ppermute | solution.py:25
  20.8 9.8 %copy-start.9 = (bf16[256,512]{1,0:T(8,128)(2,1)}, bf16[256,512]{1,0:T(8,128)(2,1)S(1)}, u32[]{:S(2)}) copy-start(bf16[256,512]{1,0:T(8,128)(2,1)S(1)} %collective-permute-done.5.refs_5_) | copy-start | bytes 786436
  20.8 17.6 %collective-permute-start.6 = (bf16[256,512]{1,0:T(8,128)(2,1)S(1)}, bf16[256,512]{1,0:T(8,128)(2,1)S(1)}, u32[]{:S(2)}, u32[]{:S(2)}) collective-permute-start(bf16[256,512]{1,0:T(8,128)(2,1)S(1)} %collective-permute-done.5.refs_5_), channel_id=1, source_target_pairs={{0,8},{4,12},{8,0},{12,4},{16,24},{20,28},{24,16},{28,20},{1,9},{5... | collective-permute-start | bytes 786440 | tf_op jit(solution)/shard_map/ppermute | solution.py:25
  20.8 21.5 %collective-permute-start = (bf16[256,512]{1,0:T(8,128)(2,1)}, bf16[256,512]{1,0:T(8,128)(2,1)S(1)}, u32[]{:S(2)}, u32[]{:S(2)}) collective-permute-start(bf16[256,512]{1,0:T(8,128)(2,1)} %refs_0_.3), channel_id=1, source_target_pairs={{0,1},{1,0},{2,3},{3,2},{4,5},{5,4},{6,7},{7,6},{8,9},{9,8},{10,11... | collective-permute-start | bytes 786440 | tf_op jit(solution)/shard_map/ppermute | solution.py:25
  22.4 8.3 %copy-start.3 = (bf16[256,512]{1,0:T(8,128)(2,1)}, bf16[256,512]{1,0:T(8,128)(2,1)S(1)}, u32[]{:S(2)}) copy-start(bf16[256,512]{1,0:T(8,128)(2,1)S(1)} %collective-permute-done.4.refs_4_.refs_5_) | copy-start | bytes 786436
  22.4 20.7 %collective-permute-start.1 = (bf16[256,512]{1,0:T(8,128)(2,1)}, bf16[256,512]{1,0:T(8,128)(2,1)S(1)}, u32[]{:S(2)}, u32[]{:S(2)}) collective-permute-start(bf16[256,512]{1,0:T(8,128)(2,1)} %refs_0_.3), channel_id=1, source_target_pairs={{0,2},{1,3},{2,0},{3,1},{4,6},{5,7},{6,4},{7,5},{8,10},{9,11},{10,... | collective-permute-start | bytes 786440 | tf_op jit(solution)/shard_map/ppermute | solution.py:25
  30.6 13.8 %collective-permute-start.2 = (bf16[256,512]{1,0:T(8,128)(2,1)}, bf16[256,512]{1,0:T(8,128)(2,1)S(1)}, u32[]{:S(2)}, u32[]{:S(2)}) collective-permute-start(bf16[256,512]{1,0:T(8,128)(2,1)} %refs_0_.3), channel_id=1, source_target_pairs={{0,3},{1,2},{2,1},{3,0},{4,7},{5,6},{6,5},{7,4},{8,11},{9,10},{10,... | collective-permute-start | bytes 786440 | tf_op jit(solution)/shard_map/ppermute | solution.py:25
  36.1 3.9 %copy-start.5 = (bf16[256,512]{1,0:T(8,128)(2,1)}, bf16[256,512]{1,0:T(8,128)(2,1)S(1)}, u32[]{:S(2)}) copy-start(bf16[256,512]{1,0:T(8,128)(2,1)S(1)} %collective-permute-done.9.refs_2_.refs_9_) | copy-start | bytes 786436
  36.2 12.2 %collective-permute-start.3 = (bf16[256,512]{1,0:T(8,128)(2,1)}, bf16[256,512]{1,0:T(8,128)(2,1)S(1)}, u32[]{:S(2)}, u32[]{:S(2)}) collective-permute-start(bf16[256,512]{1,0:T(8,128)(2,1)} %key.3), channel_id=1, source_target_pairs={{0,4},{4,0},{8,12},{12,8},{16,20},{20,16},{24,28},{28,24},{1,5},{5... | collective-permute-start | bytes 786440 | tf_op jit(solution)/shard_map/ppermute | solution.py:25
  38.4 12.8 %collective-permute-start.7 = (bf16[256,512]{1,0:T(8,128)(2,1)}, bf16[256,512]{1,0:T(8,128)(2,1)S(1)}, u32[]{:S(2)}, u32[]{:S(2)}) collective-permute-start(bf16[256,512]{1,0:T(8,128)(2,1)} %value.3), channel_id=1, source_target_pairs={{0,4},{4,0},{8,12},{12,8},{16,20},{20,16},{24,28},{28,24},{1,5},{5... | collective-permute-start | bytes 786440 | tf_op jit(solution)/shard_map/ppermute | solution.py:25
  42.3 14.5 %collective-permute-start.11 = (bf16[256,512]{1,0:T(8,128)(2,1)}, bf16[256,512]{1,0:T(8,128)(2,1)S(1)}, u32[]{:S(2)}, u32[]{:S(2)}) collective-permute-start(bf16[256,512]{1,0:T(8,128)(2,1)} %get-tuple-element.34.refs_10_), channel_id=1, source_target_pairs={{0,4},{4,0},{8,12},{12,8},{16,20},{20,16},{24,28},{28,24},{1,5},{5... | collective-permute-start | bytes 786440 | tf_op jit(solution)/shard_map/ppermute | solution.py:25
  43.0 17.3 %collective-permute-start.12 = (bf16[256,512]{1,0:T(8,128)(2,1)}, bf16[256,512]{1,0:T(8,128)(2,1)S(1)}, u32[]{:S(2)}, u32[]{:S(2)}) collective-permute-start(bf16[256,512]{1,0:T(8,128)(2,1)} %get-tuple-element.35.refs_12_), channel_id=1, source_target_pairs={{0,4},{4,0},{8,12},{12,8},{16,20},{20,16},{24,28},{28,24},{1,5},{5... | collective-permute-start | bytes 786440 | tf_op jit(solution)/shard_map/ppermute | solution.py:25
  48.4 24.0 %copy-start.4 = (bf16[256,512]{1,0:T(8,128)(2,1)S(1)}, bf16[256,512]{1,0:T(8,128)(2,1)}, u32[]{:S(2)}) copy-start(bf16[256,512]{1,0:T(8,128)(2,1)} %refs_0_.5) | copy-start | bytes 786436
  48.4 12.0 %copy-start.10 = (bf16[256,512]{1,0:T(8,128)(2,1)}, bf16[256,512]{1,0:T(8,128)(2,1)S(1)}, u32[]{:S(2)}) copy-start(bf16[256,512]{1,0:T(8,128)(2,1)S(1)} %collective-permute-done.3.refs_4_) | copy-start | bytes 786436
  51.2 9.2 %copy-start.11 = (bf16[256,512]{1,0:T(8,128)(2,1)}, bf16[256,512]{1,0:T(8,128)(2,1)S(1)}, u32[]{:S(2)}) copy-start(bf16[256,512]{1,0:T(8,128)(2,1)S(1)} %collective-permute-done.7.refs_7_) | copy-start | bytes 786436
  61.0 30.3 %copy-start.1 = (bf16[256,512]{1,0:T(8,128)(2,1)S(1)}, bf16[256,512]{1,0:T(8,128)(2,1)}, u32[]{:S(2)}) copy-start(bf16[256,512]{1,0:T(8,128)(2,1)} %shard_map.102.refs_1_) | copy-start | bytes 786436
  70.8 41.7 %copy-start.28 = (f32[32,256]{1,0:T(8,128)S(1)}, f32[32,256]{1,0:T(8,128)}, u32[]{:S(2)}) copy-start(f32[32,256]{1,0:T(8,128)} %get-tuple-element.43.refs_2_) | copy-start | bytes 98308
  70.8 9.3 %collective-permute-start.25 = (bf16[256,512]{1,0:T(8,128)(2,1)}, bf16[256,512]{1,0:T(8,128)(2,1)S(1)}, u32[]{:S(2)}, u32[]{:S(2)}) collective-permute-start(bf16[256,512]{1,0:T(8,128)(2,1)} %get-tuple-element.49), channel_id=1, source_target_pairs={{0,4},{4,0},{8,12},{12,8},{16,20},{20,16},{24,28},{28,24},{1,5},{5... | collective-permute-start | bytes 786440 | tf_op jit(solution)/shard_map/ppermute | solution.py:25
  72.4 20.4 %collective-permute-start.16 = (bf16[256,512]{1,0:T(8,128)(2,1)S(1)}, bf16[256,512]{1,0:T(8,128)(2,1)S(1)}, u32[]{:S(2)}, u32[]{:S(2)}) collective-permute-start(bf16[256,512]{1,0:T(8,128)(2,1)S(1)} %copy-done.4), channel_id=1, source_target_pairs={{0,4},{4,0},{8,12},{12,8},{16,20},{20,16},{24,28},{28,24},{1,5},{5... | collective-permute-start | bytes 786440 | tf_op jit(solution)/shard_map/ppermute | solution.py:25
  81.3 21.2 %collective-permute-start.26 = (bf16[256,512]{1,0:T(8,128)(2,1)S(1)}, bf16[256,512]{1,0:T(8,128)(2,1)S(1)}, u32[]{:S(2)}, u32[]{:S(2)}) collective-permute-start(bf16[256,512]{1,0:T(8,128)(2,1)S(1)} %fusion), channel_id=1, source_target_pairs={{0,8},{4,12},{8,0},{12,4},{16,24},{20,28},{24,16},{28,20},{1,9},{5... | collective-permute-start | bytes 786440 | tf_op jit(solution)/shard_map/ppermute | solution.py:25
  87.6 19.8 %collective-permute-start.17 = (bf16[256,512]{1,0:T(8,128)(2,1)S(1)}, bf16[256,512]{1,0:T(8,128)(2,1)S(1)}, u32[]{:S(2)}, u32[]{:S(2)}) collective-permute-start(bf16[256,512]{1,0:T(8,128)(2,1)S(1)} %copy-done.4), channel_id=1, source_target_pairs={{0,8},{4,12},{8,0},{12,4},{16,24},{20,28},{24,16},{28,20},{1,9},{5... | collective-permute-start | bytes 786440 | tf_op jit(solution)/shard_map/ppermute | solution.py:25
  87.7 24.8 %collective-permute-start.18 = (bf16[256,512]{1,0:T(8,128)(2,1)S(1)}, bf16[256,512]{1,0:T(8,128)(2,1)S(1)}, u32[]{:S(2)}, u32[]{:S(2)}) collective-permute-start(bf16[256,512]{1,0:T(8,128)(2,1)S(1)} %copy-done.4), channel_id=1, source_target_pairs={{0,16},{4,20},{8,24},{12,28},{16,0},{20,4},{24,8},{28,12},{1,17},{... | collective-permute-start | bytes 786440 | tf_op jit(solution)/shard_map/ppermute | solution.py:25
  91.3 22.9 %collective-permute-start.19 = (bf16[256,512]{1,0:T(8,128)(2,1)S(1)}, bf16[256,512]{1,0:T(8,128)(2,1)S(1)}, u32[]{:S(2)}, u32[]{:S(2)}) collective-permute-start(bf16[256,512]{1,0:T(8,128)(2,1)S(1)} %copy-done.1), channel_id=1, source_target_pairs={{0,4},{4,0},{8,12},{12,8},{16,20},{20,16},{24,28},{28,24},{1,5},{5... | collective-permute-start | bytes 786440 | tf_op jit(solution)/shard_map/ppermute | solution.py:25
  92.8 32.0 %copy-start.16 = (bf16[256,512]{1,0:T(8,128)(2,1)}, bf16[256,512]{1,0:T(8,128)(2,1)S(1)}, u32[]{:S(2)}) copy-start(bf16[256,512]{1,0:T(8,128)(2,1)S(1)} %collective-permute-done.16.refs_0_) | copy-start | bytes 786436
  92.8 21.4 %collective-permute-start.20 = (bf16[256,512]{1,0:T(8,128)(2,1)S(1)}, bf16[256,512]{1,0:T(8,128)(2,1)S(1)}, u32[]{:S(2)}, u32[]{:S(2)}) collective-permute-start(bf16[256,512]{1,0:T(8,128)(2,1)S(1)} %copy-done.1), channel_id=1, source_target_pairs={{0,8},{4,12},{8,0},{12,4},{16,24},{20,28},{24,16},{28,20},{1,9},{5... | collective-permute-start | bytes 786440 | tf_op jit(solution)/shard_map/ppermute | solution.py:25
  102.5 22.9 %collective-permute-start.21 = (bf16[256,512]{1,0:T(8,128)(2,1)S(1)}, bf16[256,512]{1,0:T(8,128)(2,1)S(1)}, u32[]{:S(2)}, u32[]{:S(2)}) collective-permute-start(bf16[256,512]{1,0:T(8,128)(2,1)S(1)} %copy-done.1), channel_id=1, source_target_pairs={{0,16},{4,20},{8,24},{12,28},{16,0},{20,4},{24,8},{28,12},{1,17},{... | collective-permute-start | bytes 786440 | tf_op jit(solution)/shard_map/ppermute | solution.py:25
  107.4 25.9 %copy-start.17 = (bf16[256,512]{1,0:T(8,128)(2,1)}, bf16[256,512]{1,0:T(8,128)(2,1)S(1)}, u32[]{:S(2)}) copy-start(bf16[256,512]{1,0:T(8,128)(2,1)S(1)} %collective-permute-done.17.refs_1_) | copy-start | bytes 786436
  107.4 34.1 %collective-permute-start.27 = (bf16[256,512]{1,0:T(8,128)(2,1)S(1)}, bf16[256,512]{1,0:T(8,128)(2,1)S(1)}, u32[]{:S(2)}, u32[]{:S(2)}) collective-permute-start(bf16[256,512]{1,0:T(8,128)(2,1)S(1)} %fusion.1), channel_id=1, source_target_pairs={{0,24},{4,28},{8,16},{12,20},{16,8},{20,12},{24,0},{28,4},{1,25},{... | collective-permute-start | bytes 786440 | tf_op jit(solution)/shard_map/ppermute | solution.py:25
  112.5 20.7 %copy-start.18 = (bf16[256,512]{1,0:T(8,128)(2,1)}, bf16[256,512]{1,0:T(8,128)(2,1)S(1)}, u32[]{:S(2)}) copy-start(bf16[256,512]{1,0:T(8,128)(2,1)S(1)} %collective-permute-done.18.refs_2_) | copy-start | bytes 786436
  112.5 12.9 %collective-permute-start.22 = (f32[32,256]{1,0:T(8,128)S(1)}, f32[32,256]{1,0:T(8,128)S(1)}, u32[]{:S(2)}, u32[]{:S(2)}) collective-permute-start(f32[32,256]{1,0:T(8,128)S(1)} %copy-done.28), channel_id=1, source_target_pairs={{0,4},{4,0},{8,12},{12,8},{16,20},{20,16},{24,28},{28,24},{1,5},{5... | collective-permute-start | bytes 98312 | tf_op jit(solution)/shard_map/ppermute | solution.py:25
  114.2 11.2 %copy-start.19 = (bf16[256,512]{1,0:T(8,128)(2,1)}, bf16[256,512]{1,0:T(8,128)(2,1)S(1)}, u32[]{:S(2)}) copy-start(bf16[256,512]{1,0:T(8,128)(2,1)S(1)} %collective-permute-done.19.refs_3_) | copy-start | bytes 786436
  114.2 18.8 %collective-permute-start.23 = (f32[32,256]{1,0:T(8,128)S(1)}, f32[32,256]{1,0:T(8,128)S(1)}, u32[]{:S(2)}, u32[]{:S(2)}) collective-permute-start(f32[32,256]{1,0:T(8,128)S(1)} %copy-done.28), channel_id=1, source_target_pairs={{0,8},{4,12},{8,0},{12,4},{16,24},{20,28},{24,16},{28,20},{1,9},{5... | collective-permute-start | bytes 98312 | tf_op jit(solution)/shard_map/ppermute | solution.py:25
  114.2 11.2 %copy-start.20 = (bf16[256,512]{1,0:T(8,128)(2,1)}, bf16[256,512]{1,0:T(8,128)(2,1)S(1)}, u32[]{:S(2)}) copy-start(bf16[256,512]{1,0:T(8,128)(2,1)S(1)} %collective-permute-done.20.refs_4_) | copy-start | bytes 786436
  114.2 19.0 %collective-permute-start.24 = (f32[32,256]{1,0:T(8,128)S(1)}, f32[32,256]{1,0:T(8,128)S(1)}, u32[]{:S(2)}, u32[]{:S(2)}) collective-permute-start(f32[32,256]{1,0:T(8,128)S(1)} %copy-done.28), channel_id=1, source_target_pairs={{0,16},{4,20},{8,24},{12,28},{16,0},{20,4},{24,8},{28,12},{1,17},{... | collective-permute-start | bytes 98312 | tf_op jit(solution)/shard_map/ppermute | solution.py:25
  124.8 16.7 %copy-start = (f32[256,512]{1,0:T(8,128)S(1)}, f32[256,512]{1,0:T(8,128)}, u32[]{:S(2)}) copy-start(f32[256,512]{1,0:T(8,128)} %get-tuple-element.48) | copy-start | bytes 1572868
  125.4 7.7 %copy-start.21 = (bf16[256,512]{1,0:T(8,128)(2,1)}, bf16[256,512]{1,0:T(8,128)(2,1)S(1)}, u32[]{:S(2)}) copy-start(bf16[256,512]{1,0:T(8,128)(2,1)S(1)} %collective-permute-done.21.refs_5_) | copy-start | bytes 786436
  125.4 17.9 %collective-permute-start.13 = (bf16[256,512]{1,0:T(8,128)(2,1)}, bf16[256,512]{1,0:T(8,128)(2,1)S(1)}, u32[]{:S(2)}, u32[]{:S(2)}) collective-permute-start(bf16[256,512]{1,0:T(8,128)(2,1)} %get-tuple-element.38), channel_id=1, source_target_pairs={{0,1},{1,0},{2,3},{3,2},{4,5},{5,4},{6,7},{7,6},{8,9},{9,8},{10,11... | collective-permute-start | bytes 786440 | tf_op jit(solution)/shard_map/ppermute | solution.py:25
  125.4 7.8 %copy-start.25 = (f32[32,256]{1,0:T(8,128)}, f32[32,256]{1,0:T(8,128)S(1)}, u32[]{:S(2)}) copy-start(f32[32,256]{1,0:T(8,128)S(1)} %collective-permute-done.22.refs_6_) | copy-start | bytes 98308
  125.4 17.8 %collective-permute-start.14 = (bf16[256,512]{1,0:T(8,128)(2,1)}, bf16[256,512]{1,0:T(8,128)(2,1)S(1)}, u32[]{:S(2)}, u32[]{:S(2)}) collective-permute-start(bf16[256,512]{1,0:T(8,128)(2,1)} %get-tuple-element.39), channel_id=1, source_target_pairs={{0,2},{1,3},{2,0},{3,1},{4,6},{5,7},{6,4},{7,5},{8,10},{9,11},{10,... | collective-permute-start | bytes 786440 | tf_op jit(solution)/shard_map/ppermute | solution.py:25
  133.0 12.5 %collective-permute-start.15 = (bf16[256,512]{1,0:T(8,128)(2,1)}, bf16[256,512]{1,0:T(8,128)(2,1)S(1)}, u32[]{:S(2)}, u32[]{:S(2)}) collective-permute-start(bf16[256,512]{1,0:T(8,128)(2,1)} %get-tuple-element.40), channel_id=1, source_target_pairs={{0,3},{1,2},{2,1},{3,0},{4,7},{5,6},{6,5},{7,4},{8,11},{9,10},{10,... | collective-permute-start | bytes 786440 | tf_op jit(solution)/shard_map/ppermute | solution.py:25
  133.8 11.8 %copy-start.8 = (f32[256,512]{1,0:T(8,128)S(1)}, f32[256,512]{1,0:T(8,128)}, u32[]{:S(2)}) copy-start(f32[256,512]{1,0:T(8,128)} %get-tuple-element.37) | copy-start | bytes 1572868
  141.6 8.8 %copy-start.7 = (bf16[256,512]{1,0:T(8,128)(2,1)}, bf16[256,512]{1,0:T(8,128)(2,1)S(1)}, u32[]{:S(2)}) copy-start(bf16[256,512]{1,0:T(8,128)(2,1)S(1)} %add_convert_fusion.kept) | copy-start | bytes 786436
  141.6 8.8 %collective-permute-start.28 = (bf16[256,512]{1,0:T(8,128)(2,1)S(1)}, bf16[256,512]{1,0:T(8,128)(2,1)S(1)}, u32[]{:S(2)}, u32[]{:S(2)}) collective-permute-start(bf16[256,512]{1,0:T(8,128)(2,1)S(1)} %add_convert_fusion.kept), channel_id=1, source_target_pairs={{0,4},{4,0},{8,12},{12,8},{16,20},{20,16},{24,28},{28,24},{1,5},{5... | collective-permute-start | bytes 786440 | tf_op jit(solution)/shard_map/ppermute | solution.py:25
  (10 other events, 12.7 us)
where the time goes:
time: 154 us
  starting transfers between devices  61.2 us (40%)
  waiting for transfers between devices  47.9 us (31%)
  Pallas kernels  37.1 us (24%)
  local copies, waits for them, and re-layouts  3.43 us (2%)
  other arithmetic  3.24 us (2%)
    ppermute x29, starting transfers between devices, swap(): lax.ppermute(shard, axis, [(i, i ^ mask) for i in range(lax.axis_size(axi...  61.2 us
    ppermute x29, waiting for transfers between devices, swap(): lax.ppermute(shard, axis, [(i, i ^ mask) for i in range(lax.axis_size(axi...  47.9 us
    pallas_call x8, Pallas kernels, call(): pl.pallas_call(kernel, in_specs=in_specs, out_specs=outs, out_shape=out_s...  34.6 us
    unnamed x58, local copies, waits for them, and re-layouts  3.43 us
  transfers between devices with their start and end apart: 29, of which 14 were waited for; matrix products, arithmetic and copies ran while one was open for 2% of the time, Pallas kernels for 16%

commit v1 on v0

--- a/solution.py
+++ b/solution.py
@@ -12,6 +12,7 @@
 HEAD_SIZE = 128
 BLOCK = 128
 STAT_ROWS = 8
+KERNEL_VMEM = 16 * 2**20
 
 
 FACTOR = 1.0 / math.sqrt(HEAD_SIZE)
@@ -28,14 +29,20 @@
 def call(kernel, out_shape, *operands, scalars=0, scratch=()):
     in_specs = [pl.BlockSpec(memory_space=pltpu.SMEM)] * scalars
     in_specs += [pl.BlockSpec(memory_space=pltpu.VMEM)] * (len(operands) - scalars)
-    outs = jax.tree.map(lambda _: pl.BlockSpec(memory_space=pltpu.VMEM), out_shape)
+    outs = [pl.BlockSpec(memory_space=pltpu.VMEM)] * len(out_shape)
+    placed = [pltpu.with_memory_space_constraint(o, pltpu.VMEM) for o in operands[scalars:]]
     return pl.pallas_call(
-        kernel, in_specs=in_specs, out_specs=outs, out_shape=out_shape, scratch_shapes=scratch
-    )(*operands)
+        kernel,
+        in_specs=in_specs,
+        out_specs=outs,
+        out_shape=out_shape,
+        scratch_shapes=scratch,
+        compiler_params=pltpu.CompilerParams(vmem_limit_bytes=KERNEL_VMEM),
+    )(*operands[:scalars], *placed)
 
 
 def like(shape, dtype=jnp.bfloat16):
-    return jax.ShapeDtypeStruct(shape, dtype)
+    return pltpu.VMEM(shape, dtype)
 
 
 def dot(a, b, dims=(((1,), (0,)), ((), ()))):
@@ -70,33 +77,52 @@
         out[...] = dot(att_ref[...], weight_ref[:, pl.ds(start, width)]).astype(out.dtype)
 
 
-def hot_kernel(masks, cols_ref, scatter_ref, *select_refs):
+def hot_kernel(masks, groups, cols_ref, scatter_ref, *outs):
     rows, slots = scatter_ref.shape
     device = lax.axis_index("ctx")
     row_ids = lax.broadcasted_iota(jnp.int32, (rows, slots), 0)
-    for mask, select_ref in zip(masks, select_refs):
-        local = cols_ref[...] - jnp.bitwise_xor(device, mask) * rows
-        chosen = (row_ids == local).astype(F32)
+
+    def local(mask):
+        return cols_ref[...] - jnp.bitwise_xor(device, mask) * rows
+
+    for mask, out in zip(masks, outs):
+        chosen = (row_ids == local(mask)).astype(F32)
         if mask == 0:
             scatter_ref[...] = chosen.astype(BF16)
-        select_ref[...] = chosen.T.astype(BF16)
-
-
-def select_kernel(count, more, *refs):
-    selects, keys, values = (refs[part * count : (part + 1) * count] for part in range(3))
-    refs = refs[3 * count :]
-    outs = refs[-2:]
-    for sources, so_far, out in zip((keys, values), refs[:-2] if more else (None, None), outs):
-        total = so_far[...].astype(F32) if more else 0.0
-        for select, source in zip(selects, sources):
-            total = total + dot(select[...], source[...])
-        out[...] = total.astype(BF16)
-
-
-def select_globals(selects, keys, values, so_far=()):
-    shape = like((selects[0].shape[0], keys[0].shape[1]))
-    kernel = functools.partial(select_kernel, len(selects), bool(so_far))
-    return call(kernel, [shape, shape], *selects, *keys, *values, *so_far)
+        out[...] = chosen.T.astype(BF16)
+    for group, out in zip(groups, outs[len(masks) :]):
+        owned = 0.0
+        for mask in group:
+            at = jnp.broadcast_to(local(mask), (out.shape[1], slots))
+            owned = owned + jnp.logical_and(at >= 0, at < rows).astype(F32)
+        out[...] = owned.T
+
+
+def select_kernel(count, *refs):
+    total = dot(refs[0][...], refs[count][...])
+    for select, source in zip(refs[1:count], refs[count + 1 : -1]):
+        total = total + dot(select[...], source[...])
+    refs[-1][...] = total.astype(BF16)
+
+
+def select_globals(selects, sources):
+    shape = like((selects[0].shape[0], sources[0].shape[1]))
+    kernel = functools.partial(select_kernel, len(selects))
+    return call(kernel, [shape], *selects, *sources)[0]
+
+
+def merged(have, got, owned):
+    return (have.astype(F32) + owned * got.astype(F32)).astype(BF16)
+
+
+def merge_kernel(have, got, owned, out):
+    for start in range(0, out.shape[1], HEAD_SIZE):
+        part = pl.ds(start, HEAD_SIZE)
+        out[:, part] = merged(have[:, part], got[:, part], owned[...])
+
+
+def merge(have, got, owned):
+    return call(merge_kernel, [like(have.shape)], have, got, owned)[0]
 
 
 def query_kernel(strides, glob_parts, cols_ref, *refs):
@@ -104,7 +130,7 @@
     refs = refs[4:]
     far_keys, far_values, refs = refs[:strides], refs[strides : 2 * strides], refs[2 * strides :]
     glob_keys, glob_values = refs[:glob_parts], refs[glob_parts : 2 * glob_parts]
-    att_out, query_out, keep_out, send_out, stat_out, stats = refs[2 * glob_parts :]
+    att_out, query_out, keep_out, send_out, stat_out, stats = refs[-6:]
     blocks = query.shape[0] // BLOCK
     heads = query.shape[1] // HEAD_SIZE
     near = (strides + 1) * BLOCK
@@ -114,8 +140,14 @@
 
     def one_head(head, _):
         part = columns_of(head)
-        glob_key = sum((ref[:, part] for ref in glob_keys[1:]), glob_keys[0][:, part])
-        glob_value = sum((ref[:, part] for ref in glob_values[1:]), glob_values[0][:, part])
+        if glob_parts == 1:
+            glob_key, glob_value = glob_keys[0][:, part], glob_values[0][:, part]
+        else:
+            owned = refs[2 * glob_parts][...]
+            glob_key, glob_value = (
+                merged(have[:, part], got[:, part], owned)
+                for have, got in (glob_keys, glob_values)
+            )
         glob_grads, glob_weights = [], []
         for i in range(blocks):
             rows = pl.ds(i * BLOCK, BLOCK)
@@ -165,7 +197,9 @@
         stat_out[:, rows] = stats[rows, :].T[: stat_out.shape[0]]
 
 
-def query_side(cols, query, grad, key, value, far_keys, far_values, glob_keys, glob_values):
+def query_side(
+    cols, query, grad, key, value, far_keys, far_values, glob_keys, glob_values, owned=()
+):
     rows, width = query.shape
     strides = len(far_keys)
     slots = glob_keys[0].shape[0]
@@ -188,6 +222,7 @@
         *far_values,
         *glob_keys,
         *glob_values,
+        *owned,
         scalars=1,
         scratch=[pltpu.VMEM((rows, BLOCK), F32)],
     )
@@ -260,71 +295,59 @@
 
 
 def finish(scatter, key, value, kept, got):
-    rows, width = key.shape
-    slots = kept.shape[0]
-    part = lambda count: pl.BlockSpec((count, width // 2), lambda h: (0, h))
-    shape = like((rows, width))
-    return pl.pallas_call(
-        final_kernel,
-        grid=(2,),
-        in_specs=[pl.BlockSpec((rows, slots), lambda h: (0, 0))]
-        + [part(rows)] * 2
-        + [part(slots)] * 2,
-        out_specs=[part(rows)] * 2,
-        out_shape=[shape, shape],
-        name="finish",
-    )(scatter, key, value, kept, got)
+    shape = jax.ShapeDtypeStruct(key.shape, BF16)
+    return call(final_kernel, [shape, shape], scatter, key, value, kept, got)
 
 
 def per_device(query_act, key_act, value_act, out_weight, cotangent, butterfly_cols, global_cols):
     strides = butterfly_cols.shape[1]
     groups = lax.axis_size("head")
-    ring = strides == 3 and lax.axis_size("ctx") == 1 << strides
+    cube = strides == 3 and lax.axis_size("ctx") == 1 << strides
     cols = butterfly_cols.T
     slots = global_cols.shape[0]
     rows, width = key_act.shape
     masks = [1 << s for s in range(strides)]
-    held = (0, 2, 6, 4) if ring else (0,)
-
-    scatter, *selects = call(
-        functools.partial(hot_kernel, held),
-        [like((rows, slots))] + [like((slots, rows))] * len(held),
+    held = (0, *masks) if cube else (0,)
+    owners = ((3, 5), (6, 7)) if cube else ()
+
+    scatter, *hot = call(
+        functools.partial(hot_kernel, held, owners),
+        [like((rows, slots))]
+        + [like((slots, rows))] * len(held)
+        + [like((slots, HEAD_SIZE), F32)] * len(owners),
         global_cols.reshape(1, -1),
     )
-    direct = (2, 6, 1) if ring else masks
-    near = {m: (swap(key_act, "ctx", m), swap(value_act, "ctx", m)) for m in direct}
+    selects, owned = hot[: len(held)], hot[len(held) :]
+    near_keys = [key_act] + [swap(key_act, "ctx", m) for m in masks]
+    near_values = [value_act] + [swap(value_act, "ctx", m) for m in masks]
     pieces = [cotangent] + [swap(cotangent, "head", m) for m in range(1, groups)]
-    near[0] = (key_act, value_act)
-    if ring:
-        near[4] = (swap(near[6][0], "ctx", 2), swap(near[2][1], "ctx", 6))
-        first, last = held[:-1], held[-1]
-        so_far = select_globals(
-            selects[:-1], [near[m][0] for m in first], [near[m][1] for m in first]
-        )
-        glob_key, glob_value = select_globals(
-            selects[-1:], [near[last][0]], [near[last][1]], so_far
-        )
-        glob_keys = [glob_key, swap(glob_key, "ctx", 1)]
-        glob_values = [glob_value, swap(glob_value, "ctx", 1)]
+    far_query = [swap(query_act, "ctx", m) for m in masks]
+    if cube:
+        glob = []
+        for near in (near_keys, near_values):
+            have = select_globals(selects, near)
+            have = merge(have, swap(have, "ctx", 1), owned[0])
+            glob.append([have, swap(have, "ctx", 2)])
+        glob_keys, glob_values = glob
     else:
-        parts = select_globals(selects, [key_act], [value_act])
-        glob_keys, glob_values = ([part] for part in lax.psum(tuple(parts), "ctx"))
-    far_query = {m: swap(query_act, "ctx", m) for m in masks}
-    attn_grad = call(grad_kernel, like((rows, width)), out_weight, *pieces)
-    far_grad = {m: swap(attn_grad, "ctx", m) for m in masks}
+        parts = (select_globals(selects, [key_act]), select_globals(selects, [value_act]))
+        glob_keys, glob_values = ([part] for part in lax.psum(parts, "ctx"))
+    attn_grad = call(grad_kernel, [like((rows, width))], out_weight, *pieces)[0]
+    far_grad = [swap(attn_grad, "ctx", m) for m in masks]
     attention, query_grad, keep, send, stats = query_side(
         cols,
         query_act,
         attn_grad,
         key_act,
         value_act,
-        [near[m][0] for m in masks],
-        [near[m][1] for m in masks],
+        near_keys[1:],
+        near_values[1:],
         glob_keys,
         glob_values,
-    )
-    far_stats = {m: swap(stats, "ctx", m) for m in masks}
-    if ring:
+        owned[1:],
+    )
+    far_stats = [swap(stats, "ctx", m) for m in masks]
+    if cube:
         total = keep + swap(send, "ctx", 1).astype(F32)
         total = total + swap(total.astype(BF16), "ctx", 2).astype(F32)
         total = total + swap(total.astype(BF16), "ctx", 6).astype(F32)
@@ -346,14 +369,7 @@
         layer_out = layer_out + swap(terms[m], "head", m).astype(F32)
     so_far = key_side((-1,), cols, key_act, value_act, [query_act], [attn_grad], [stats])
     key_sum, value_sum = key_side(
-        tuple(range(strides)),
-        cols,
-        key_act,
-        value_act,
-        [far_query[m] for m in masks],
-        [far_grad[m] for m in masks],
-        [far_stats[m] for m in masks],
-        so_far,
+        tuple(range(strides)), cols, key_act, value_act, far_query, far_grad, far_stats, so_far
     )
     key_grad, value_grad = finish(scatter, key_sum, value_sum, kept, got)
     return (layer_out.astype(BF16), query_grad, key_grad, value_grad)

time: 154 us -> 121 us (0.79)
  starting transfers between devices: 61.2 us -> 34.5 us
  Pallas kernels: 37.1 us -> 19.3 us
  waiting for transfers between devices: 47.9 us -> 61.6 us
  other arithmetic: 3.24 us -> 1.21 us
    ppermute x29, starting transfers between devices: 61.2 us -> 34.5 us  [swap(): lax.ppermute(shard, axis, [(i, i ^ mask) for i in range(lax.axis_size(axi...]
    pallas_call x8 -> x11, Pallas kernels: 34.6 us -> 19.3 us  [call(): pl.pallas_call(kernel, in_specs=in_specs, out_specs=outs, out_shape=out_s...]
    ppermute x29, waiting for transfers between devices: 47.9 us -> 61.6 us  [swap(): lax.ppermute(shard, axis, [(i, i ^ mask) for i in range(lax.axis_size(axi...]
    pallas_call x1 -> x0, Pallas kernels: 2.51 us -> none  [finish(): pl.pallas_call(final_kernel, grid=(2,), in_specs=[pl.BlockSpec((rows, slo...]
    unnamed x58 -> x19, local copies, waits for them, and re-layouts: 3.43 us -> 3.32 us
  transfers between devices with their start and end apart: 29 -> 29, of which waited for: 14 -> 18; matrix products, arithmetic and copies ran while one was open for 2% -> 2% of each run, Pallas kernels for 16% -> 9%
where the time goes in v1:
time: 121 us
  waiting for transfers between devices  61.6 us (51%)
  starting transfers between devices  34.5 us (29%)
  Pallas kernels  19.3 us (16%)
  local copies, waits for them, and re-layouts  3.32 us (3%)
  other arithmetic  1.21 us (1%)
    ppermute x29, waiting for transfers between devices, swap(): lax.ppermute(shard, axis, [(i, i ^ mask) for i in range(lax.axis_size(axi...  61.6 us
    ppermute x29, starting transfers between devices, swap(): lax.ppermute(shard, axis, [(i, i ^ mask) for i in range(lax.axis_size(axi...  34.5 us
    pallas_call x11, Pallas kernels, call(): pl.pallas_call(kernel, in_specs=in_specs, out_specs=outs, out_shape=out_s...  19.3 us
    unnamed x19, local copies, waits for them, and re-layouts  3.32 us
  transfers between devices with their start and end apart: 29, of which 18 were waited for; matrix products, arithmetic and copies ran while one was open for 2% of the time, Pallas kernels for 9%

profile of v1, /device:TPU:0, one launch (start us, length us, event | category | flops | bytes accessed | tf_op | source)
XLA Modules:
  0.0 120.7 jit_solution(4894511270995998964)
XLA Ops:
  0.6 3.1 %collective-permute-start.6 = (bf16[256,512]{1,0:T(8,128)(2,1)}, bf16[256,512]{1,0:T(8,128)(2,1)S(1)}, u32[]{:S(2)}, u32[]{:S(2)}) collective-permute-start(bf16[256,512]{1,0:T(8,128)(2,1)} %value.3), channel_id=1, source_target_pairs={{0,4},{4,0},{8,12},{12,8},{16,20},{20,16},{24,28},{28,24},{1,5},{5... | collective-permute-start | bytes 786440 | tf_op jit(solution)/shard_map/ppermute | solution.py:26
  3.7 1.6 %collective-permute-start.7 = (bf16[256,512]{1,0:T(8,128)(2,1)}, bf16[256,512]{1,0:T(8,128)(2,1)S(1)}, u32[]{:S(2)}, u32[]{:S(2)}) collective-permute-start(bf16[256,512]{1,0:T(8,128)(2,1)} %value.3), channel_id=1, source_target_pairs={{0,8},{4,12},{8,0},{12,4},{16,24},{20,28},{24,16},{28,20},{1,9},{5... | collective-permute-start | bytes 786440 | tf_op jit(solution)/shard_map/ppermute | solution.py:26
  5.3 2.6 %collective-permute-start.8 = (bf16[256,512]{1,0:T(8,128)(2,1)}, bf16[256,512]{1,0:T(8,128)(2,1)S(1)}, u32[]{:S(2)}, u32[]{:S(2)}) collective-permute-start(bf16[256,512]{1,0:T(8,128)(2,1)} %value.3), channel_id=1, source_target_pairs={{0,16},{4,20},{8,24},{12,28},{16,0},{20,4},{24,8},{28,12},{1,17},{... | collective-permute-start | bytes 786440 | tf_op jit(solution)/shard_map/ppermute | solution.py:26
  7.9 0.5 collective-permute-start.3
  8.8 1.9 %collective-permute-done.6.refs_5_.refs_7_ = bf16[256,512]{1,0:T(8,128)(2,1)S(1)} collective-permute-done((bf16[256,512]{1,0:T(8,128)(2,1)}, bf16[256,512]{1,0:T(8,128)(2,1)S(1)}, u32[]{:S(2)}, u32[]{:S(2)}) %collective-permute-start.6) | collective-permute-done | bytes 262176 | tf_op jit(solution)/shard_map/ppermute | solution.py:26
  10.8 3.4 %collective-permute-start.5 = (bf16[256,512]{1,0:T(8,128)(2,1)}, bf16[256,512]{1,0:T(8,128)(2,1)S(1)}, u32[]{:S(2)}, u32[]{:S(2)}) collective-permute-start(bf16[256,512]{1,0:T(8,128)(2,1)} %key.3), channel_id=1, source_target_pairs={{0,16},{4,20},{8,24},{12,28},{16,0},{20,4},{24,8},{28,12},{1,17},{... | collective-permute-start | bytes 786440 | tf_op jit(solution)/shard_map/ppermute | solution.py:26
  14.1 0.7 copy-done.8
  15.1 4.0 %collective-permute-done.7.refs_6_.refs_8_ = bf16[256,512]{1,0:T(8,128)(2,1)S(1)} collective-permute-done((bf16[256,512]{1,0:T(8,128)(2,1)}, bf16[256,512]{1,0:T(8,128)(2,1)S(1)}, u32[]{:S(2)}, u32[]{:S(2)}) %collective-permute-start.7) | collective-permute-done | bytes 262176 | tf_op jit(solution)/shard_map/ppermute | solution.py:26
  19.1 1.6 %collective-permute-done.8.refs_7_.refs_9_ = bf16[256,512]{1,0:T(8,128)(2,1)S(1)} collective-permute-done((bf16[256,512]{1,0:T(8,128)(2,1)}, bf16[256,512]{1,0:T(8,128)(2,1)S(1)}, u32[]{:S(2)}, u32[]{:S(2)}) %collective-permute-start.8) | collective-permute-done | bytes 262176 | tf_op jit(solution)/shard_map/ppermute | solution.py:26
  20.7 0.9 copy-done.3
  22.2 6.2 %collective-permute-done.4.refs_6_.refs_5_ = bf16[256,512]{1,0:T(8,128)(2,1)S(1)} collective-permute-done((bf16[256,512]{1,0:T(8,128)(2,1)}, bf16[256,512]{1,0:T(8,128)(2,1)S(1)}, u32[]{:S(2)}, u32[]{:S(2)}) %collective-permute-start.4) | collective-permute-done | bytes 262176 | tf_op jit(solution)/shard_map/ppermute | solution.py:26
  28.4 2.4 %collective-permute-done.5.refs_7_.refs_6_ = bf16[256,512]{1,0:T(8,128)(2,1)S(1)} collective-permute-done((bf16[256,512]{1,0:T(8,128)(2,1)}, bf16[256,512]{1,0:T(8,128)(2,1)S(1)}, u32[]{:S(2)}, u32[]{:S(2)}) %collective-permute-start.5) | collective-permute-done | bytes 262176 | tf_op jit(solution)/shard_map/ppermute | solution.py:26
  30.8 0.9 copy-done.1
  32.2 0.6 collective-permute-start.9
  32.8 1.5 %collective-permute-start.1 = (bf16[256,512]{1,0:T(8,128)(2,1)S(1)}, bf16[256,512]{1,0:T(8,128)(2,1)S(1)}, u32[]{:S(2)}, u32[]{:S(2)}) collective-permute-start(bf16[256,512]{1,0:T(8,128)(2,1)S(1)} %copy-done.6), channel_id=1, source_target_pairs={{0,2},{1,3},{2,0},{3,1},{4,6},{5,7},{6,4},{7,5},{8,10},{9,11},{10,... | collective-permute-start | bytes 786440 | tf_op jit(solution)/shard_map/ppermute | solution.py:26
  35.3 3.4 %collective-permute-done.9.got = bf16[256,512]{1,0:T(8,128)(2,1)S(1)} collective-permute-done((bf16[256,512]{1,0:T(8,128)(2,1)S(1)}, bf16[256,512]{1,0:T(8,128)(2,1)S(1)}, u32[]{:S(2)}, u32[]{:S(2)}) %collective-permute-start.9) | collective-permute-done | bytes 262176 | tf_op jit(solution)/shard_map/ppermute | solution.py:26
  38.8 1.0 collective-permute-start.10
  39.7 2.2 %collective-permute-done.1.refs_2_ = bf16[256,512]{1,0:T(8,128)(2,1)S(1)} collective-permute-done((bf16[256,512]{1,0:T(8,128)(2,1)S(1)}, bf16[256,512]{1,0:T(8,128)(2,1)S(1)}, u32[]{:S(2)}, u32[]{:S(2)}) %collective-permute-start.1) | collective-permute-done | bytes 262176 | tf_op jit(solution)/shard_map/ppermute | solution.py:26
  42.0 4.7 %collective-permute-done.2.refs_3_ = bf16[256,512]{1,0:T(8,128)(2,1)S(1)} collective-permute-done((bf16[256,512]{1,0:T(8,128)(2,1)S(1)}, bf16[256,512]{1,0:T(8,128)(2,1)S(1)}, u32[]{:S(2)}, u32[]{:S(2)}) %collective-permute-start.2) | collective-permute-done | bytes 262176 | tf_op jit(solution)/shard_map/ppermute | solution.py:26
  46.7 0.7 shard_map.102.refs_1_
  47.4 1.6 %collective-permute-done.10.refs_11_ = bf16[256,512]{1,0:T(8,128)(2,1)S(1)} collective-permute-done((bf16[256,512]{1,0:T(8,128)(2,1)S(1)}, bf16[256,512]{1,0:T(8,128)(2,1)S(1)}, u32[]{:S(2)}, u32[]{:S(2)}) %collective-permute-start.10) | collective-permute-done | bytes 262176 | tf_op jit(solution)/shard_map/ppermute | solution.py:26
  49.0 7.5 %shard_map.108 = (bf16[256,512]{1,0:T(8,128)(2,1)S(1)}, bf16[256,512]{1,0:T(8,128)(2,1)S(1)}, f32[256,512]{1,0:T(8,128)S(1)}, bf16[256,512]{1,0:T(8,128)(2,1)S(1)}, f32[32,256]{1,0:T(8,128)S(1)}) custom-call(s32[3,16]{1,0:T(4,128)S(1)} %bitcast.2, bf16[256,512]{1,0:T(8,128)(2,1)S(1)} %copy-done.5, bf16[256,512]{1,0:T(8,128)(2,1)S(1)} %shard_map.102.refs_1_, ...), custom_call_target="tpu_custom_call" | custom-call | tf_op jit(solution)/shard_map/pallas_call | solution.py:34
  56.5 1.6 %collective-permute-start.25 = (bf16[256,512]{1,0:T(8,128)(2,1)S(1)}, bf16[256,512]{1,0:T(8,128)(2,1)S(1)}, u32[]{:S(2)}, u32[]{:S(2)}) collective-permute-start(bf16[256,512]{1,0:T(8,128)(2,1)S(1)} %get-tuple-element.45), channel_id=1, source_target_pairs={{0,4},{4,0},{8,12},{12,8},{16,20},{20,16},{24,28},{28,24},{1,5},{5... | collective-permute-start | bytes 786440 | tf_op jit(solution)/shard_map/ppermute | solution.py:26
  58.1 0.5 collective-permute-start.16
  58.6 7.1 %collective-permute-done.25 = bf16[256,512]{1,0:T(8,128)(2,1)S(1)} collective-permute-done((bf16[256,512]{1,0:T(8,128)(2,1)S(1)}, bf16[256,512]{1,0:T(8,128)(2,1)S(1)}, u32[]{:S(2)}, u32[]{:S(2)}) %collective-permute-start.25) | collective-permute-done | bytes 262176 | tf_op jit(solution)/shard_map/ppermute | solution.py:26
  66.4 1.6 %collective-permute-start.17 = (bf16[256,512]{1,0:T(8,128)(2,1)S(1)}, bf16[256,512]{1,0:T(8,128)(2,1)S(1)}, u32[]{:S(2)}, u32[]{:S(2)}) collective-permute-start(bf16[256,512]{1,0:T(8,128)(2,1)S(1)} %copy-done.5), channel_id=1, source_target_pairs={{0,8},{4,12},{8,0},{12,4},{16,24},{20,28},{24,16},{28,20},{1,9},{5... | collective-permute-start | bytes 786440 | tf_op jit(solution)/shard_map/ppermute | solution.py:26
  68.0 1.3 %collective-permute-start.18 = (bf16[256,512]{1,0:T(8,128)(2,1)S(1)}, bf16[256,512]{1,0:T(8,128)(2,1)S(1)}, u32[]{:S(2)}, u32[]{:S(2)}) collective-permute-start(bf16[256,512]{1,0:T(8,128)(2,1)S(1)} %copy-done.5), channel_id=1, source_target_pairs={{0,16},{4,20},{8,24},{12,28},{16,0},{20,4},{24,8},{28,12},{1,17},{... | collective-permute-start | bytes 786440 | tf_op jit(solution)/shard_map/ppermute | solution.py:26
  69.2 1.5 %collective-permute-start.19 = (bf16[256,512]{1,0:T(8,128)(2,1)S(1)}, bf16[256,512]{1,0:T(8,128)(2,1)S(1)}, u32[]{:S(2)}, u32[]{:S(2)}) collective-permute-start(bf16[256,512]{1,0:T(8,128)(2,1)S(1)} %shard_map.102.refs_1_), channel_id=1, source_target_pairs={{0,4},{4,0},{8,12},{12,8},{16,20},{20,16},{24,28},{28,24},{1,5},{5... | collective-permute-start | bytes 786440 | tf_op jit(solution)/shard_map/ppermute | solution.py:26
  71.1 1.4 %collective-permute-start.20 = (bf16[256,512]{1,0:T(8,128)(2,1)S(1)}, bf16[256,512]{1,0:T(8,128)(2,1)S(1)}, u32[]{:S(2)}, u32[]{:S(2)}) collective-permute-start(bf16[256,512]{1,0:T(8,128)(2,1)S(1)} %shard_map.102.refs_1_), channel_id=1, source_target_pairs={{0,8},{4,12},{8,0},{12,4},{16,24},{20,28},{24,16},{28,20},{1,9},{5... | collective-permute-start | bytes 786440 | tf_op jit(solution)/shard_map/ppermute | solution.py:26
  72.5 9.6 %collective-permute-done.26 = bf16[256,512]{1,0:T(8,128)(2,1)S(1)} collective-permute-done((bf16[256,512]{1,0:T(8,128)(2,1)S(1)}, bf16[256,512]{1,0:T(8,128)(2,1)S(1)}, u32[]{:S(2)}, u32[]{:S(2)}) %collective-permute-start.26) | collective-permute-done | bytes 262176 | tf_op jit(solution)/shard_map/ppermute | solution.py:26
  82.1 0.5 collective-permute-start.21
  82.7 5.1 %collective-permute-done.17.refs_1_ = bf16[256,512]{1,0:T(8,128)(2,1)S(1)} collective-permute-done((bf16[256,512]{1,0:T(8,128)(2,1)S(1)}, bf16[256,512]{1,0:T(8,128)(2,1)S(1)}, u32[]{:S(2)}, u32[]{:S(2)}) %collective-permute-start.17) | collective-permute-done | bytes 262176 | tf_op jit(solution)/shard_map/ppermute | solution.py:26
  87.8 2.7 %collective-permute-start.27 = (bf16[256,512]{1,0:T(8,128)(2,1)S(1)}, bf16[256,512]{1,0:T(8,128)(2,1)S(1)}, u32[]{:S(2)}, u32[]{:S(2)}) collective-permute-start(bf16[256,512]{1,0:T(8,128)(2,1)S(1)} %fusion.1), channel_id=1, source_target_pairs={{0,24},{4,28},{8,16},{12,20},{16,8},{20,12},{24,0},{28,4},{1,25},{... | collective-permute-start | bytes 786440 | tf_op jit(solution)/shard_map/ppermute | solution.py:26
  90.5 1.5 %collective-permute-start.22 = (f32[32,256]{1,0:T(8,128)S(1)}, f32[32,256]{1,0:T(8,128)S(1)}, u32[]{:S(2)}, u32[]{:S(2)}) collective-permute-start(f32[32,256]{1,0:T(8,128)S(1)} %get-tuple-element.39.refs_2_), channel_id=1, source_target_pairs={{0,4},{4,0},{8,12},{12,8},{16,20},{20,16},{24,28},{28,24},{1,5},{5... | collective-permute-start | bytes 98312 | tf_op jit(solution)/shard_map/ppermute | solution.py:26
  92.0 1.5 %collective-permute-done.20.refs_4_ = bf16[256,512]{1,0:T(8,128)(2,1)S(1)} collective-permute-done((bf16[256,512]{1,0:T(8,128)(2,1)S(1)}, bf16[256,512]{1,0:T(8,128)(2,1)S(1)}, u32[]{:S(2)}, u32[]{:S(2)}) %collective-permute-start.20) | collective-permute-done | bytes 262176 | tf_op jit(solution)/shard_map/ppermute | solution.py:26
  93.5 2.3 %collective-permute-start.24 = (f32[32,256]{1,0:T(8,128)S(1)}, f32[32,256]{1,0:T(8,128)S(1)}, u32[]{:S(2)}, u32[]{:S(2)}) collective-permute-start(f32[32,256]{1,0:T(8,128)S(1)} %get-tuple-element.39.refs_2_), channel_id=1, source_target_pairs={{0,16},{4,20},{8,24},{12,28},{16,0},{20,4},{24,8},{28,12},{1,17},{... | collective-permute-start | bytes 98312 | tf_op jit(solution)/shard_map/ppermute | solution.py:26
  95.9 2.5 %shard_map.110 = (f32[256,512]{1,0:T(8,128)S(1)}, f32[256,512]{1,0:T(8,128)S(1)}) custom-call(s32[3,16]{1,0:T(4,128)S(1)} %bitcast.3, bf16[256,512]{1,0:T(8,128)(2,1)S(1)} %copy-done.2, bf16[256,512]{1,0:T(8,128)(2,1)S(1)} %copy-done.4, bf16[256,512]{1,0:T(8,128)(2,1)S(1)} %copy-done.5, bf16[256,512]{1,0:T(8,128)(2,1)S(1)} %shard_map.102.refs_1_, ...), custom_call_target="tpu_custom_call" | custom-call | tf_op jit(solution)/shard_map/pallas_call | solution.py:34
  98.4 0.7 shard_map.109
  99.1 0.7 copy.11
  99.8 3.8 %collective-permute-done.21.refs_5_ = bf16[256,512]{1,0:T(8,128)(2,1)S(1)} collective-permute-done((bf16[256,512]{1,0:T(8,128)(2,1)S(1)}, bf16[256,512]{1,0:T(8,128)(2,1)S(1)}, u32[]{:S(2)}, u32[]{:S(2)}) %collective-permute-start.21) | collective-permute-done | bytes 262176 | tf_op jit(solution)/shard_map/ppermute | solution.py:26
  103.7 1.5 %collective-permute-start.14 = (bf16[256,512]{1,0:T(8,128)(2,1)S(1)}, bf16[256,512]{1,0:T(8,128)(2,1)S(1)}, u32[]{:S(2)}, u32[]{:S(2)}) collective-permute-start(bf16[256,512]{1,0:T(8,128)(2,1)S(1)} %get-tuple-element.35), channel_id=1, source_target_pairs={{0,2},{1,3},{2,0},{3,1},{4,6},{5,7},{6,4},{7,5},{8,10},{9,11},{10,... | collective-permute-start | bytes 786440 | tf_op jit(solution)/shard_map/ppermute | solution.py:26
  105.5 1.3 %collective-permute-done.24.refs_8_ = f32[32,256]{1,0:T(8,128)S(1)} collective-permute-done((f32[32,256]{1,0:T(8,128)S(1)}, f32[32,256]{1,0:T(8,128)S(1)}, u32[]{:S(2)}, u32[]{:S(2)}) %collective-permute-start.24) | collective-permute-done | bytes 32800 | tf_op jit(solution)/shard_map/ppermute | solution.py:26
  106.8 5.3 %shard_map.111 = (f32[256,512]{1,0:T(8,128)S(1)}, f32[256,512]{1,0:T(8,128)S(1)}) custom-call(s32[3,16]{1,0:T(4,128)S(1)} %bitcast.4, bf16[256,512]{1,0:T(8,128)(2,1)S(1)} %copy-done.2, bf16[256,512]{1,0:T(8,128)(2,1)S(1)} %copy-done.4, bf16[256,512]{1,0:T(8,128)(2,1)S(1)} %collective-permute-done.16.refs_0_, ...), custom_call_target="tpu_custom_call" | custom-call | tf_op jit(solution)/shard_map/pallas_call | solution.py:34
  112.3 1.6 %collective-permute-start.28 = (bf16[256,512]{1,0:T(8,128)(2,1)S(1)}, bf16[256,512]{1,0:T(8,128)(2,1)S(1)}, u32[]{:S(2)}, u32[]{:S(2)}) collective-permute-start(bf16[256,512]{1,0:T(8,128)(2,1)S(1)} %add_convert_fusion.kept), channel_id=1, source_target_pairs={{0,4},{4,0},{8,12},{12,8},{16,20},{20,16},{24,28},{28,24},{1,5},{5... | collective-permute-start | bytes 786440 | tf_op jit(solution)/shard_map/ppermute | solution.py:26
  113.9 3.7 %collective-permute-done.15 = bf16[256,512]{1,0:T(8,128)(2,1)S(1)} collective-permute-done((bf16[256,512]{1,0:T(8,128)(2,1)S(1)}, bf16[256,512]{1,0:T(8,128)(2,1)S(1)}, u32[]{:S(2)}, u32[]{:S(2)}) %collective-permute-start.15) | collective-permute-done | bytes 262176 | tf_op jit(solution)/shard_map/ppermute | solution.py:26
  117.5 0.8 add_convert_fusion.1
  118.4 1.2 collective-permute-done.28.got
  119.6 1.1 shard_map.112
  (44 shorter events, 4.4 us)
Async XLA Ops:
  0.6 10.1 %collective-permute-start.6 = (bf16[256,512]{1,0:T(8,128)(2,1)}, bf16[256,512]{1,0:T(8,128)(2,1)S(1)}, u32[]{:S(2)}, u32[]{:S(2)}) collective-permute-start(bf16[256,512]{1,0:T(8,128)(2,1)} %value.3), channel_id=1, source_target_pairs={{0,4},{4,0},{8,12},{12,8},{16,20},{20,16},{24,28},{28,24},{1,5},{5... | collective-permute-start | bytes 786440 | tf_op jit(solution)/shard_map/ppermute | solution.py:26
  3.7 15.4 %collective-permute-start.7 = (bf16[256,512]{1,0:T(8,128)(2,1)}, bf16[256,512]{1,0:T(8,128)(2,1)S(1)}, u32[]{:S(2)}, u32[]{:S(2)}) collective-permute-start(bf16[256,512]{1,0:T(8,128)(2,1)} %value.3), channel_id=1, source_target_pairs={{0,8},{4,12},{8,0},{12,4},{16,24},{20,28},{24,16},{28,20},{1,9},{5... | collective-permute-start | bytes 786440 | tf_op jit(solution)/shard_map/ppermute | solution.py:26
  5.3 15.4 %collective-permute-start.8 = (bf16[256,512]{1,0:T(8,128)(2,1)}, bf16[256,512]{1,0:T(8,128)(2,1)S(1)}, u32[]{:S(2)}, u32[]{:S(2)}) collective-permute-start(bf16[256,512]{1,0:T(8,128)(2,1)} %value.3), channel_id=1, source_target_pairs={{0,16},{4,20},{8,24},{12,28},{16,0},{20,4},{24,8},{28,12},{1,17},{... | collective-permute-start | bytes 786440 | tf_op jit(solution)/shard_map/ppermute | solution.py:26
  7.9 14.3 %collective-permute-start.3 = (bf16[256,512]{1,0:T(8,128)(2,1)}, bf16[256,512]{1,0:T(8,128)(2,1)S(1)}, u32[]{:S(2)}, u32[]{:S(2)}) collective-permute-start(bf16[256,512]{1,0:T(8,128)(2,1)} %key.3), channel_id=1, source_target_pairs={{0,4},{4,0},{8,12},{12,8},{16,20},{20,16},{24,28},{28,24},{1,5},{5... | collective-permute-start | bytes 786440 | tf_op jit(solution)/shard_map/ppermute | solution.py:26
  8.4 20.0 %collective-permute-start.4 = (bf16[256,512]{1,0:T(8,128)(2,1)}, bf16[256,512]{1,0:T(8,128)(2,1)S(1)}, u32[]{:S(2)}, u32[]{:S(2)}) collective-permute-start(bf16[256,512]{1,0:T(8,128)(2,1)} %key.3), channel_id=1, source_target_pairs={{0,8},{4,12},{8,0},{12,4},{16,24},{20,28},{24,16},{28,20},{1,9},{5... | collective-permute-start | bytes 786440 | tf_op jit(solution)/shard_map/ppermute | solution.py:26
  10.8 20.1 %collective-permute-start.5 = (bf16[256,512]{1,0:T(8,128)(2,1)}, bf16[256,512]{1,0:T(8,128)(2,1)S(1)}, u32[]{:S(2)}, u32[]{:S(2)}) collective-permute-start(bf16[256,512]{1,0:T(8,128)(2,1)} %key.3), channel_id=1, source_target_pairs={{0,16},{4,20},{8,24},{12,28},{16,0},{20,4},{24,8},{28,12},{1,17},{... | collective-permute-start | bytes 786440 | tf_op jit(solution)/shard_map/ppermute | solution.py:26
  14.1 0.7 copy-start.8
  20.7 1.0 copy-start.3
  21.7 11.1 %copy-start.6 = (bf16[256,512]{1,0:T(8,128)(2,1)S(1)}, bf16[256,512]{1,0:T(8,128)(2,1)}, u32[]{:S(2)}) copy-start(bf16[256,512]{1,0:T(8,128)(2,1)} %refs_0_.3) | copy-start | bytes 786436
  22.1 24.6 %copy-start = (bf16[512,2048]{1,0:T(8,128)(2,1)S(1)}, bf16[512,2048]{1,0:T(8,128)(2,1)}, u32[]{:S(2)}) copy-start(bf16[512,2048]{1,0:T(8,128)(2,1)} %weight_ref.3) | copy-start | bytes 6291460
  22.1 12.5 %collective-permute-start.11 = (bf16[256,512]{1,0:T(8,128)(2,1)S(1)}, bf16[256,512]{1,0:T(8,128)(2,1)S(1)}, u32[]{:S(2)}, u32[]{:S(2)}) collective-permute-start(bf16[256,512]{1,0:T(8,128)(2,1)S(1)} %shard_map.106.have), channel_id=1, source_target_pairs={{0,4},{4,0},{8,12},{12,8},{16,20},{20,16},{24,28},{28,24},{1,5},{5... | collective-permute-start | bytes 786440 | tf_op jit(solution)/shard_map/ppermute | solution.py:26
  30.8 1.0 copy-start.1
  32.2 6.4 %collective-permute-start.9 = (bf16[256,512]{1,0:T(8,128)(2,1)S(1)}, bf16[256,512]{1,0:T(8,128)(2,1)S(1)}, u32[]{:S(2)}, u32[]{:S(2)}) collective-permute-start(bf16[256,512]{1,0:T(8,128)(2,1)S(1)} %shard_map.104.have), channel_id=1, source_target_pairs={{0,4},{4,0},{8,12},{12,8},{16,20},{20,16},{24,28},{28,24},{1,5},{5... | collective-permute-start | bytes 786440 | tf_op jit(solution)/shard_map/ppermute | solution.py:26
  32.8 7.0 %collective-permute-start = (bf16[256,512]{1,0:T(8,128)(2,1)S(1)}, bf16[256,512]{1,0:T(8,128)(2,1)S(1)}, u32[]{:S(2)}, u32[]{:S(2)}) collective-permute-start(bf16[256,512]{1,0:T(8,128)(2,1)S(1)} %copy-done.6), channel_id=1, source_target_pairs={{0,1},{1,0},{2,3},{3,2},{4,5},{5,4},{6,7},{7,6},{8,9},{9,8},{10,11... | collective-permute-start | bytes 786440 | tf_op jit(solution)/shard_map/ppermute | solution.py:26
  32.8 9.2 %collective-permute-start.1 = (bf16[256,512]{1,0:T(8,128)(2,1)S(1)}, bf16[256,512]{1,0:T(8,128)(2,1)S(1)}, u32[]{:S(2)}, u32[]{:S(2)}) collective-permute-start(bf16[256,512]{1,0:T(8,128)(2,1)S(1)} %copy-done.6), channel_id=1, source_target_pairs={{0,2},{1,3},{2,0},{3,1},{4,6},{5,7},{6,4},{7,5},{8,10},{9,11},{10,... | collective-permute-start | bytes 786440 | tf_op jit(solution)/shard_map/ppermute | solution.py:26
  34.3 12.4 %collective-permute-start.2 = (bf16[256,512]{1,0:T(8,128)(2,1)S(1)}, bf16[256,512]{1,0:T(8,128)(2,1)S(1)}, u32[]{:S(2)}, u32[]{:S(2)}) collective-permute-start(bf16[256,512]{1,0:T(8,128)(2,1)S(1)} %copy-done.6), channel_id=1, source_target_pairs={{0,3},{1,2},{2,1},{3,0},{4,7},{5,6},{6,5},{7,4},{8,11},{9,10},{10,... | collective-permute-start | bytes 786440 | tf_op jit(solution)/shard_map/ppermute | solution.py:26
  34.7 14.2 %copy-start.2 = (bf16[256,512]{1,0:T(8,128)(2,1)S(1)}, bf16[256,512]{1,0:T(8,128)(2,1)}, u32[]{:S(2)}) copy-start(bf16[256,512]{1,0:T(8,128)(2,1)} %key.3) | copy-start | bytes 786436
  34.8 14.2 %copy-start.4 = (bf16[256,512]{1,0:T(8,128)(2,1)S(1)}, bf16[256,512]{1,0:T(8,128)(2,1)}, u32[]{:S(2)}) copy-start(bf16[256,512]{1,0:T(8,128)(2,1)} %value.3) | copy-start | bytes 786436
  34.8 14.2 %copy-start.5 = (bf16[256,512]{1,0:T(8,128)(2,1)S(1)}, bf16[256,512]{1,0:T(8,128)(2,1)}, u32[]{:S(2)}) copy-start(bf16[256,512]{1,0:T(8,128)(2,1)} %refs_0_.5) | copy-start | bytes 786436
  34.8 14.2 %copy-start.7 = (s32[16,3]{0,1:T(4,128)S(1)}, s32[16,3]{0,1:T(4,128)}, u32[]{:S(2)}) copy-start(s32[16,3]{0,1:T(4,128)} %param.12) | copy-start | bytes 580
  34.8 12.6 %collective-permute-start.12 = (bf16[256,512]{1,0:T(8,128)(2,1)S(1)}, bf16[256,512]{1,0:T(8,128)(2,1)S(1)}, u32[]{:S(2)}, u32[]{:S(2)}) collective-permute-start(bf16[256,512]{1,0:T(8,128)(2,1)S(1)} %shard_map.107.refs_12_), channel_id=1, source_target_pairs={{0,8},{4,12},{8,0},{12,4},{16,24},{20,28},{24,16},{28,20},{1,9},{5... | collective-permute-start | bytes 786440 | tf_op jit(solution)/shard_map/ppermute | solution.py:26
  38.8 10.2 %collective-permute-start.10 = (bf16[256,512]{1,0:T(8,128)(2,1)S(1)}, bf16[256,512]{1,0:T(8,128)(2,1)S(1)}, u32[]{:S(2)}, u32[]{:S(2)}) collective-permute-start(bf16[256,512]{1,0:T(8,128)(2,1)S(1)} %shard_map.105.refs_10_), channel_id=1, source_target_pairs={{0,8},{4,12},{8,0},{12,4},{16,24},{20,28},{24,16},{28,20},{1,9},{5... | collective-permute-start | bytes 786440 | tf_op jit(solution)/shard_map/ppermute | solution.py:26
  56.5 9.2 %collective-permute-start.25 = (bf16[256,512]{1,0:T(8,128)(2,1)S(1)}, bf16[256,512]{1,0:T(8,128)(2,1)S(1)}, u32[]{:S(2)}, u32[]{:S(2)}) collective-permute-start(bf16[256,512]{1,0:T(8,128)(2,1)S(1)} %get-tuple-element.45), channel_id=1, source_target_pairs={{0,4},{4,0},{8,12},{12,8},{16,20},{20,16},{24,28},{28,24},{1,5},{5... | collective-permute-start | bytes 786440 | tf_op jit(solution)/shard_map/ppermute | solution.py:26
  58.1 13.0 %collective-permute-start.16 = (bf16[256,512]{1,0:T(8,128)(2,1)S(1)}, bf16[256,512]{1,0:T(8,128)(2,1)S(1)}, u32[]{:S(2)}, u32[]{:S(2)}) collective-permute-start(bf16[256,512]{1,0:T(8,128)(2,1)S(1)} %copy-done.5), channel_id=1, source_target_pairs={{0,4},{4,0},{8,12},{12,8},{16,20},{20,16},{24,28},{28,24},{1,5},{5... | collective-permute-start | bytes 786440 | tf_op jit(solution)/shard_map/ppermute | solution.py:26
  65.9 16.2 %collective-permute-start.26 = (bf16[256,512]{1,0:T(8,128)(2,1)S(1)}, bf16[256,512]{1,0:T(8,128)(2,1)S(1)}, u32[]{:S(2)}, u32[]{:S(2)}) collective-permute-start(bf16[256,512]{1,0:T(8,128)(2,1)S(1)} %fusion), channel_id=1, source_target_pairs={{0,8},{4,12},{8,0},{12,4},{16,24},{20,28},{24,16},{28,20},{1,9},{5... | collective-permute-start | bytes 786440 | tf_op jit(solution)/shard_map/ppermute | solution.py:26
  66.4 21.5 %collective-permute-start.17 = (bf16[256,512]{1,0:T(8,128)(2,1)S(1)}, bf16[256,512]{1,0:T(8,128)(2,1)S(1)}, u32[]{:S(2)}, u32[]{:S(2)}) collective-permute-start(bf16[256,512]{1,0:T(8,128)(2,1)S(1)} %copy-done.5), channel_id=1, source_target_pairs={{0,8},{4,12},{8,0},{12,4},{16,24},{20,28},{24,16},{28,20},{1,9},{5... | collective-permute-start | bytes 786440 | tf_op jit(solution)/shard_map/ppermute | solution.py:26
  68.0 22.6 %collective-permute-start.18 = (bf16[256,512]{1,0:T(8,128)(2,1)S(1)}, bf16[256,512]{1,0:T(8,128)(2,1)S(1)}, u32[]{:S(2)}, u32[]{:S(2)}) collective-permute-start(bf16[256,512]{1,0:T(8,128)(2,1)S(1)} %copy-done.5), channel_id=1, source_target_pairs={{0,16},{4,20},{8,24},{12,28},{16,0},{20,4},{24,8},{28,12},{1,17},{... | collective-permute-start | bytes 786440 | tf_op jit(solution)/shard_map/ppermute | solution.py:26
  69.2 22.8 %collective-permute-start.19 = (bf16[256,512]{1,0:T(8,128)(2,1)S(1)}, bf16[256,512]{1,0:T(8,128)(2,1)S(1)}, u32[]{:S(2)}, u32[]{:S(2)}) collective-permute-start(bf16[256,512]{1,0:T(8,128)(2,1)S(1)} %shard_map.102.refs_1_), channel_id=1, source_target_pairs={{0,4},{4,0},{8,12},{12,8},{16,20},{20,16},{24,28},{28,24},{1,5},{5... | collective-permute-start | bytes 786440 | tf_op jit(solution)/shard_map/ppermute | solution.py:26
  71.1 22.4 %collective-permute-start.20 = (bf16[256,512]{1,0:T(8,128)(2,1)S(1)}, bf16[256,512]{1,0:T(8,128)(2,1)S(1)}, u32[]{:S(2)}, u32[]{:S(2)}) collective-permute-start(bf16[256,512]{1,0:T(8,128)(2,1)S(1)} %shard_map.102.refs_1_), channel_id=1, source_target_pairs={{0,8},{4,12},{8,0},{12,4},{16,24},{20,28},{24,16},{28,20},{1,9},{5... | collective-permute-start | bytes 786440 | tf_op jit(solution)/shard_map/ppermute | solution.py:26
  82.1 21.6 %collective-permute-start.21 = (bf16[256,512]{1,0:T(8,128)(2,1)S(1)}, bf16[256,512]{1,0:T(8,128)(2,1)S(1)}, u32[]{:S(2)}, u32[]{:S(2)}) collective-permute-start(bf16[256,512]{1,0:T(8,128)(2,1)S(1)} %shard_map.102.refs_1_), channel_id=1, source_target_pairs={{0,16},{4,20},{8,24},{12,28},{16,0},{20,4},{24,8},{28,12},{1,17},{... | collective-permute-start | bytes 786440 | tf_op jit(solution)/shard_map/ppermute | solution.py:26
  87.8 24.3 %collective-permute-start.27 = (bf16[256,512]{1,0:T(8,128)(2,1)S(1)}, bf16[256,512]{1,0:T(8,128)(2,1)S(1)}, u32[]{:S(2)}, u32[]{:S(2)}) collective-permute-start(bf16[256,512]{1,0:T(8,128)(2,1)S(1)} %fusion.1), channel_id=1, source_target_pairs={{0,24},{4,28},{8,16},{12,20},{16,8},{20,12},{24,0},{28,4},{1,25},{... | collective-permute-start | bytes 786440 | tf_op jit(solution)/shard_map/ppermute | solution.py:26
  90.5 13.1 %collective-permute-start.22 = (f32[32,256]{1,0:T(8,128)S(1)}, f32[32,256]{1,0:T(8,128)S(1)}, u32[]{:S(2)}, u32[]{:S(2)}) collective-permute-start(f32[32,256]{1,0:T(8,128)S(1)} %get-tuple-element.39.refs_2_), channel_id=1, source_target_pairs={{0,4},{4,0},{8,12},{12,8},{16,20},{20,16},{24,28},{28,24},{1,5},{5... | collective-permute-start | bytes 98312 | tf_op jit(solution)/shard_map/ppermute | solution.py:26
  92.0 13.1 %collective-permute-start.23 = (f32[32,256]{1,0:T(8,128)S(1)}, f32[32,256]{1,0:T(8,128)S(1)}, u32[]{:S(2)}, u32[]{:S(2)}) collective-permute-start(f32[32,256]{1,0:T(8,128)S(1)} %get-tuple-element.39.refs_2_), channel_id=1, source_target_pairs={{0,8},{4,12},{8,0},{12,4},{16,24},{20,28},{24,16},{28,20},{1,9},{5... | collective-permute-start | bytes 98312 | tf_op jit(solution)/shard_map/ppermute | solution.py:26
  93.5 13.3 %collective-permute-start.24 = (f32[32,256]{1,0:T(8,128)S(1)}, f32[32,256]{1,0:T(8,128)S(1)}, u32[]{:S(2)}, u32[]{:S(2)}) collective-permute-start(f32[32,256]{1,0:T(8,128)S(1)} %get-tuple-element.39.refs_2_), channel_id=1, source_target_pairs={{0,16},{4,20},{8,24},{12,28},{16,0},{20,4},{24,8},{28,12},{1,17},{... | collective-permute-start | bytes 98312 | tf_op jit(solution)/shard_map/ppermute | solution.py:26
  103.7 10.2 %collective-permute-start.13 = (bf16[256,512]{1,0:T(8,128)(2,1)S(1)}, bf16[256,512]{1,0:T(8,128)(2,1)S(1)}, u32[]{:S(2)}, u32[]{:S(2)}) collective-permute-start(bf16[256,512]{1,0:T(8,128)(2,1)S(1)} %get-tuple-element.34), channel_id=1, source_target_pairs={{0,1},{1,0},{2,3},{3,2},{4,5},{5,4},{6,7},{7,6},{8,9},{9,8},{10,11... | collective-permute-start | bytes 786440 | tf_op jit(solution)/shard_map/ppermute | solution.py:26
  103.7 10.2 %collective-permute-start.14 = (bf16[256,512]{1,0:T(8,128)(2,1)S(1)}, bf16[256,512]{1,0:T(8,128)(2,1)S(1)}, u32[]{:S(2)}, u32[]{:S(2)}) collective-permute-start(bf16[256,512]{1,0:T(8,128)(2,1)S(1)} %get-tuple-element.35), channel_id=1, source_target_pairs={{0,2},{1,3},{2,0},{3,1},{4,6},{5,7},{6,4},{7,5},{8,10},{9,11},{10,... | collective-permute-start | bytes 786440 | tf_op jit(solution)/shard_map/ppermute | solution.py:26
  105.2 12.4 %collective-permute-start.15 = (bf16[256,512]{1,0:T(8,128)(2,1)S(1)}, bf16[256,512]{1,0:T(8,128)(2,1)S(1)}, u32[]{:S(2)}, u32[]{:S(2)}) collective-permute-start(bf16[256,512]{1,0:T(8,128)(2,1)S(1)} %get-tuple-element.36), channel_id=1, source_target_pairs={{0,3},{1,2},{2,1},{3,0},{4,7},{5,6},{6,5},{7,4},{8,11},{9,10},{10,... | collective-permute-start | bytes 786440 | tf_op jit(solution)/shard_map/ppermute | solution.py:26
  112.3 7.3 %collective-permute-start.28 = (bf16[256,512]{1,0:T(8,128)(2,1)S(1)}, bf16[256,512]{1,0:T(8,128)(2,1)S(1)}, u32[]{:S(2)}, u32[]{:S(2)}) collective-permute-start(bf16[256,512]{1,0:T(8,128)(2,1)S(1)} %add_convert_fusion.kept), channel_id=1, source_target_pairs={{0,4},{4,0},{8,12},{12,8},{16,20},{20,16},{24,28},{28,24},{1,5},{5... | collective-permute-start | bytes 786440 | tf_op jit(solution)/shard_map/ppermute | solution.py:26

commit v2 on v1

--- a/solution.py
+++ b/solution.py
@@ -111,121 +111,148 @@
     return call(kernel, [shape], *selects, *sources)[0]
 
 
-def merged(have, got, owned):
-    return (have.astype(F32) + owned * got.astype(F32)).astype(BF16)
+def merged(parts, owned, at):
+    total = parts[0][:, at].astype(F32)
+    for part, mask in zip(parts[1:], owned):
+        total = total + mask[...] * part[:, at].astype(F32)
+    return total.astype(BF16)
 
 
 def merge_kernel(have, got, owned, out):
     for start in range(0, out.shape[1], HEAD_SIZE):
         part = pl.ds(start, HEAD_SIZE)
-        out[:, part] = merged(have[:, part], got[:, part], owned[...])
+        out[:, part] = merged((have, got), (owned,), part)
 
 
 def merge(have, got, owned):
     return call(merge_kernel, [like(have.shape)], have, got, owned)[0]
 
 
-def query_kernel(strides, glob_parts, cols_ref, *refs):
-    query, grad, own_key, own_value = refs[:4]
-    refs = refs[4:]
-    far_keys, far_values, refs = refs[:strides], refs[strides : 2 * strides], refs[2 * strides :]
-    glob_keys, glob_values = refs[:glob_parts], refs[glob_parts : 2 * glob_parts]
-    att_out, query_out, keep_out, send_out, stat_out, stats = refs[-6:]
-    blocks = query.shape[0] // BLOCK
-    heads = query.shape[1] // HEAD_SIZE
+def near_at(strides, device, blocks, i, cols_ref, own, far, part):
+    picked = [
+        far[s][
+            block_at(cols_ref[s, device * blocks + i] - jnp.bitwise_xor(device, 1 << s) * blocks),
+            part,
+        ]
+        for s in range(strides)
+    ]
+    return jnp.concatenate([own[pl.ds(i * BLOCK, BLOCK), part]] + picked, 0)
+
+
+def put_columns(ref, rows, head, columns):
+    held = ref[rows, :]
+    lane = lax.broadcasted_iota(jnp.int32, held.shape, 1)
+    for place, column in enumerate(columns):
+        held = jnp.where(lane == head * STAT_ROWS + place, column, held)
+    ref[rows, :] = held
+
+
+def take_column(ref, rows, head, place):
+    held = ref[rows, :]
+    lane = lax.broadcasted_iota(jnp.int32, held.shape, 1)
+    return jnp.sum(jnp.where(lane == head * STAT_ROWS + place, held, 0.0), axis=1, keepdims=True)
+
+
+def near_kernel(strides, cols_ref, query, grad, *refs):
+    own_key, own_value = refs[:2]
+    far_keys, far_values = refs[2 : 2 + strides], refs[2 + strides : 2 + 2 * strides]
+    exponent_out, prob_out, stats = refs[-3:]
+    blocks, heads = query.shape[0] // BLOCK, query.shape[1] // HEAD_SIZE
     near = (strides + 1) * BLOCK
     device = lax.axis_index("ctx")
-    odd = jnp.bitwise_and(device, 1) == 1
-    lane = lax.broadcasted_iota(jnp.int32, (BLOCK, BLOCK), 1)
 
     def one_head(head, _):
         part = columns_of(head)
-        if glob_parts == 1:
-            glob_key, glob_value = glob_keys[0][:, part], glob_values[0][:, part]
-        else:
-            owned = refs[2 * glob_parts][...]
-            glob_key, glob_value = (
-                merged(have[:, part], got[:, part], owned)
-                for have, got in (glob_keys, glob_values)
-            )
-        glob_grads, glob_weights = [], []
+        wide = pl.ds(pl.multiple_of(head * near, near), near)
         for i in range(blocks):
             rows = pl.ds(i * BLOCK, BLOCK)
-            picks = [
-                block_at(
-                    cols_ref[s, device * blocks + i] - jnp.bitwise_xor(device, 1 << s) * blocks
-                )
-                for s in range(strides)
-            ]
-            keys = jnp.concatenate(
-                [own_key[rows, part]]
-                + [far_keys[s][picks[s], part] for s in range(strides)]
-                + [glob_key],
-                0,
-            )
-            values = jnp.concatenate(
-                [own_value[rows, part]]
-                + [far_values[s][picks[s], part] for s in range(strides)]
-                + [glob_value],
-                0,
-            )
+            keys = near_at(strides, device, blocks, i, cols_ref, own_key, far_keys, part)
+            values = near_at(strides, device, blocks, i, cols_ref, own_value, far_values, part)
             scores = dot(query[rows, part], keys, NT) * FACTOR
             top = jnp.max(scores, axis=1, keepdims=True)
             exponent = jnp.exp(scores - top)
-            scale = 1.0 / jnp.sum(exponent, axis=1, keepdims=True)
-            weights = exponent * scale
-            rounded = weights.astype(BF16)
-            att_out[rows, part] = dot(rounded, values).astype(BF16)
             prob_grad = dot(grad[rows, part], values, NT)
-            delta = jnp.sum(weights * prob_grad, axis=1, keepdims=True)
-            score_grad = (weights * (prob_grad - delta)).astype(BF16)
-            query_out[rows, part] = (dot(score_grad, keys) * FACTOR).astype(BF16)
-            glob_grads.append(score_grad[:, near:])
-            glob_weights.append(rounded[:, near:])
-            held = stats[rows, :]
-            for place, column in enumerate((top, scale, delta)):
-                held = jnp.where(lane == head * STAT_ROWS + place, column, held)
-            stats[rows, :] = held
-        key_term = dot(jnp.concatenate(glob_grads, 0), query[:, part], TN)
-        value_term = dot(jnp.concatenate(glob_weights, 0), grad[:, part], TN)
+            exponent_out[rows, wide] = exponent
+            prob_out[rows, wide] = prob_grad
+            total = jnp.sum(exponent, axis=1, keepdims=True)
+            weighted = jnp.sum(exponent * prob_grad, axis=1, keepdims=True)
+            put_columns(stats, rows, head, (top, total, weighted))
+
+    lax.fori_loop(0, heads, one_head, None, unroll=2)
+
+
+def glob_kernel(key_parts, value_parts, query, grad, near_stats, *refs):
+    keys_in, refs = refs[:key_parts], refs[key_parts:]
+    values_in, refs = refs[:value_parts], refs[value_parts:]
+    key_masks, refs = refs[: key_parts - 1], refs[key_parts - 1 :]
+    value_masks, refs = refs[: value_parts - 1], refs[value_parts - 1 :]
+    keep_out, send_out, stat_out, rest_out, weight_out, score_out, key_out, value_out, stats = refs
+    heads, slots = query.shape[1] // HEAD_SIZE, keep_out.shape[0]
+    odd = jnp.bitwise_and(lax.axis_index("ctx"), 1) == 1
+    every = pl.ds(0, query.shape[0])
+
+    def one_head(head, _):
+        part = columns_of(head)
+        wide = pl.ds(pl.multiple_of(head * slots, slots), slots)
+        keys = merged(keys_in, key_masks, part)
+        values = merged(values_in, value_masks, part)
+        key_out[:, part] = keys
+        value_out[:, part] = values
+        near_top, near_total, near_weighted = (
+            take_column(near_stats, every, head, place) for place in range(3)
+        )
+        scores = dot(query[:, part], keys, NT) * FACTOR
+        prob_grad = dot(grad[:, part], values, NT)
+        top = jnp.maximum(near_top, jnp.max(scores, axis=1, keepdims=True))
+        exponent = jnp.exp(scores - top)
+        shrink = jnp.exp(near_top - top)
+        scale = 1.0 / (shrink * near_total + jnp.sum(exponent, axis=1, keepdims=True))
+        weights = exponent * scale
+        near_scale = shrink * scale
+        delta = near_scale * near_weighted + jnp.sum(weights * prob_grad, axis=1, keepdims=True)
+        score_grad = (weights * (prob_grad - delta)).astype(BF16)
+        rounded = weights.astype(BF16)
+        weight_out[:, wide] = rounded
+        score_out[:, wide] = score_grad
+        key_term = dot(score_grad, query[:, part], TN)
+        value_term = dot(rounded, grad[:, part], TN)
         keep_out[:, part] = jnp.where(odd, value_term, key_term)
         send_out[:, part] = jnp.where(odd, key_term, value_term).astype(BF16)
-
-    lax.fori_loop(0, heads, one_head, None)
-    for i in range(blocks):
-        rows = pl.ds(i * BLOCK, BLOCK)
+        put_columns(stats, every, head, (top, scale, delta))
+        put_columns(rest_out, every, head, (near_scale, delta))
+
+    lax.fori_loop(0, heads, one_head, None, unroll=2)
+    for start in range(0, query.shape[0], BLOCK):
+        rows = pl.ds(start, BLOCK)
         stat_out[:, rows] = stats[rows, :].T[: stat_out.shape[0]]
 
 
-def query_side(
-    cols, query, grad, key, value, far_keys, far_values, glob_keys, glob_values, owned=()
-):
-    rows, width = query.shape
-    strides = len(far_keys)
-    slots = glob_keys[0].shape[0]
-    shapes = [
-        like((rows, width)),
-        like((rows, width)),
-        like((slots, width), F32),
-        like((slots, width)),
-        like((width // HEAD_SIZE * STAT_ROWS, rows), F32),
-    ]
-    return call(
-        functools.partial(query_kernel, strides, len(glob_keys)),
-        shapes,
-        cols,
-        query,
-        grad,
-        key,
-        value,
-        *far_keys,
-        *far_values,
-        *glob_keys,
-        *glob_values,
-        *owned,
-        scalars=1,
-        scratch=[pltpu.VMEM((rows, BLOCK), F32)],
-    )
+def rest_kernel(strides, cols_ref, exponents, probs, rest, weights_in, scores_in, *refs):
+    glob_key, glob_value, own_key, own_value = refs[:4]
+    far_keys, far_values = refs[4 : 4 + strides], refs[4 + strides : 4 + 2 * strides]
+    att_out, query_out = refs[-2:]
+    blocks, heads = own_key.shape[0] // BLOCK, own_key.shape[1] // HEAD_SIZE
+    near, slots = (strides + 1) * BLOCK, glob_key.shape[0]
+    device = lax.axis_index("ctx")
+
+    def one_head(head, _):
+        part = columns_of(head)
+        wide = pl.ds(pl.multiple_of(head * near, near), near)
+        glob = pl.ds(pl.multiple_of(head * slots, slots), slots)
+        for i in range(blocks):
+            rows = pl.ds(i * BLOCK, BLOCK)
+            keys = near_at(strides, device, blocks, i, cols_ref, own_key, far_keys, part)
+            values = near_at(strides, device, blocks, i, cols_ref, own_value, far_values, part)
+            near_scale, delta = (take_column(rest, rows, head, place) for place in range(2))
+            weights = exponents[rows, wide] * near_scale
+            score_grad = (weights * (probs[rows, wide] - delta)).astype(BF16)
+            attention = dot(weights.astype(BF16), values)
+            attention = attention + dot(weights_in[rows, glob], glob_value[:, part])
+            att_out[rows, part] = attention.astype(BF16)
+            query_sum = dot(score_grad, keys) + dot(scores_in[rows, glob], glob_key[:, part])
+            query_out[rows, part] = (query_sum * FACTOR).astype(BF16)
+
+    lax.fori_loop(0, heads, one_head, None, unroll=2)
 
 
 def key_kernel(sources, cols_ref, key, value, *refs):
@@ -308,7 +335,7 @@
     rows, width = key_act.shape
     masks = [1 << s for s in range(strides)]
     held = (0, *masks) if cube else (0,)
-    owners = ((3, 5), (6, 7)) if cube else ()
+    owners = ((3, 5), (6, 7), (6,), (7,)) if cube else ()
 
     scatter, *hot = call(
         functools.partial(hot_kernel, held, owners),
@@ -322,29 +349,65 @@
     near_values = [value_act] + [swap(value_act, "ctx", m) for m in masks]
     pieces = [cotangent] + [swap(cotangent, "head", m) for m in range(1, groups)]
     far_query = [swap(query_act, "ctx", m) for m in masks]
+    key_masks, value_masks = [], []
     if cube:
-        glob = []
-        for near in (near_keys, near_values):
-            have = select_globals(selects, near)
-            have = merge(have, swap(have, "ctx", 1), owned[0])
-            glob.append([have, swap(have, "ctx", 2)])
-        glob_keys, glob_values = glob
+        have = select_globals(selects, near_keys)
+        have = merge(have, swap(have, "ctx", 1), owned[0])
+        glob_keys, key_masks = [have, swap(have, "ctx", 2)], owned[1:2]
+        have = select_globals(selects, near_values)
+        glob_values = [have] + [swap(have, "ctx", m) for m in (1, 2, 3)]
+        value_masks = [owned[0], owned[2], owned[3]]
     else:
         parts = (select_globals(selects, [key_act]), select_globals(selects, [value_act]))
         glob_keys, glob_values = ([part] for part in lax.psum(parts, "ctx"))
     attn_grad = call(grad_kernel, [like((rows, width))], out_weight, *pieces)[0]
     far_grad = [swap(attn_grad, "ctx", m) for m in masks]
-    attention, query_grad, keep, send, stats = query_side(
+    near_all = [key_act, value_act, *near_keys[1:], *near_values[1:]]
+    heads = width // HEAD_SIZE
+    near = (strides + 1) * BLOCK
+    exponents, probs, near_stats = call(
+        functools.partial(near_kernel, strides),
+        [like((rows, heads * near), F32)] * 2 + [like((rows, BLOCK), F32)],
         cols,
         query_act,
         attn_grad,
-        key_act,
-        value_act,
-        near_keys[1:],
-        near_values[1:],
-        glob_keys,
-        glob_values,
-        owned[1:],
+        *near_all,
+        scalars=1,
+    )
+    keep, send, stats, rest, weights, scores, glob_key, glob_value = call(
+        functools.partial(glob_kernel, len(glob_keys), len(glob_values)),
+        [
+            like((slots, width), F32),
+            like((slots, width)),
+            like((heads * STAT_ROWS, rows), F32),
+            like((rows, BLOCK), F32),
+            like((rows, heads * slots)),
+            like((rows, heads * slots)),
+            like((slots, width)),
+            like((slots, width)),
+        ],
+        query_act,
+        attn_grad,
+        near_stats,
+        *glob_keys,
+        *glob_values,
+        *key_masks,
+        *value_masks,
+        scratch=[pltpu.VMEM((rows, BLOCK), F32)],
+    )
+    attention, query_grad = call(
+        functools.partial(rest_kernel, strides),
+        [like((rows, width)), jax.ShapeDtypeStruct((rows, width), BF16)],
+        cols,
+        exponents,
+        probs,
+        rest,
+        weights,
+        scores,
+        glob_key,
+        glob_value,
+        *near_all,
+        scalars=1,
     )
     far_stats = [swap(stats, "ctx", m) for m in masks]
     if cube:

time: 121 us -> 115 us (0.950)
  waiting for transfers between devices: 61.6 us -> 53 us
  starting transfers between devices: 34.5 us -> 37.7 us
    ppermute x29 -> x30, waiting for transfers between devices: 61.6 us -> 53 us  [swap(): lax.ppermute(shard, axis, [(i, i ^ mask) for i in range(lax.axis_size(axi...]
    ppermute x29 -> x30, starting transfers between devices: 34.5 us -> 37.7 us  [swap(): lax.ppermute(shard, axis, [(i, i ^ mask) for i in range(lax.axis_size(axi...]
    unnamed x19 -> x18, local copies, waits for them, and re-layouts: 3.32 us -> 2.6 us
    pallas_call x11 -> x12, Pallas kernels: 19.3 us -> 19.2 us  [call(): pl.pallas_call(kernel, in_specs=in_specs, out_specs=outs, out_shape=out_s...]
  transfers between devices with their start and end apart: 29 -> 30, of which waited for: 18 -> 19; matrix products, arithmetic and copies ran while one was open for 2% -> 1% of each run, Pallas kernels for 9% -> 13%
where the time goes in v2:
time: 115 us
  waiting for transfers between devices  53 us (46%)
  starting transfers between devices  37.7 us (33%)
  Pallas kernels  19.2 us (17%)
  local copies, waits for them, and re-layouts  2.6 us (2%)
  other arithmetic  1.23 us (1%)
    ppermute x30, waiting for transfers between devices, swap(): lax.ppermute(shard, axis, [(i, i ^ mask) for i in range(lax.axis_size(axi...  53 us
    ppermute x30, starting transfers between devices, swap(): lax.ppermute(shard, axis, [(i, i ^ mask) for i in range(lax.axis_size(axi...  37.7 us
    pallas_call x12, Pallas kernels, call(): pl.pallas_call(kernel, in_specs=in_specs, out_specs=outs, out_shape=out_s...  19.2 us
    unnamed x18, local copies, waits for them, and re-layouts  2.6 us
  transfers between devices with their start and end apart: 30, of which 19 were waited for; matrix products, arithmetic and copies ran while one was open for 1% of the time, Pallas kernels for 13%

profile of v2, /device:TPU:0, one launch (start us, length us, event | category | flops | bytes accessed | tf_op | source)
XLA Modules:
  0.0 114.5 jit_solution(17172270698372727011)
XLA Ops:
  0.6 3.1 %collective-permute-start.3 = (bf16[256,512]{1,0:T(8,128)(2,1)}, bf16[256,512]{1,0:T(8,128)(2,1)S(1)}, u32[]{:S(2)}, u32[]{:S(2)}) collective-permute-start(bf16[256,512]{1,0:T(8,128)(2,1)} %key.3), channel_id=1, source_target_pairs={{0,4},{4,0},{8,12},{12,8},{16,20},{20,16},{24,28},{28,24},{1,5},{5... | collective-permute-start | bytes 786440 | tf_op jit(solution)/shard_map/ppermute | solution.py:26
  3.7 1.6 %collective-permute-start.4 = (bf16[256,512]{1,0:T(8,128)(2,1)}, bf16[256,512]{1,0:T(8,128)(2,1)S(1)}, u32[]{:S(2)}, u32[]{:S(2)}) collective-permute-start(bf16[256,512]{1,0:T(8,128)(2,1)} %key.3), channel_id=1, source_target_pairs={{0,8},{4,12},{8,0},{12,4},{16,24},{20,28},{24,16},{28,20},{1,9},{5... | collective-permute-start | bytes 786440 | tf_op jit(solution)/shard_map/ppermute | solution.py:26
  5.3 2.6 %collective-permute-start.5 = (bf16[256,512]{1,0:T(8,128)(2,1)}, bf16[256,512]{1,0:T(8,128)(2,1)S(1)}, u32[]{:S(2)}, u32[]{:S(2)}) collective-permute-start(bf16[256,512]{1,0:T(8,128)(2,1)} %key.3), channel_id=1, source_target_pairs={{0,16},{4,20},{8,24},{12,28},{16,0},{20,4},{24,8},{28,12},{1,17},{... | collective-permute-start | bytes 786440 | tf_op jit(solution)/shard_map/ppermute | solution.py:26
  7.9 0.5 collective-permute-start.6
  8.8 0.7 copy-done.8
  9.8 0.9 collective-permute-done.3.refs_2_.refs_5_.refs_4_
  10.8 3.4 %collective-permute-start.8 = (bf16[256,512]{1,0:T(8,128)(2,1)}, bf16[256,512]{1,0:T(8,128)(2,1)S(1)}, u32[]{:S(2)}, u32[]{:S(2)}) collective-permute-start(bf16[256,512]{1,0:T(8,128)(2,1)} %value.3), channel_id=1, source_target_pairs={{0,16},{4,20},{8,24},{12,28},{16,0},{20,4},{24,8},{28,12},{1,17},{... | collective-permute-start | bytes 786440 | tf_op jit(solution)/shard_map/ppermute | solution.py:26
  14.1 4.9 %collective-permute-done.4.refs_3_.refs_6_.refs_5_ = bf16[256,512]{1,0:T(8,128)(2,1)S(1)} collective-permute-done((bf16[256,512]{1,0:T(8,128)(2,1)}, bf16[256,512]{1,0:T(8,128)(2,1)S(1)}, u32[]{:S(2)}, u32[]{:S(2)}) %collective-permute-start.4) | collective-permute-done | bytes 262176 | tf_op jit(solution)/shard_map/ppermute | solution.py:26
  19.1 1.6 %collective-permute-done.5.refs_4_.refs_7_.refs_6_ = bf16[256,512]{1,0:T(8,128)(2,1)S(1)} collective-permute-done((bf16[256,512]{1,0:T(8,128)(2,1)}, bf16[256,512]{1,0:T(8,128)(2,1)S(1)}, u32[]{:S(2)}, u32[]{:S(2)}) %collective-permute-start.5) | collective-permute-done | bytes 262176 | tf_op jit(solution)/shard_map/ppermute | solution.py:26
  20.7 0.9 copy-done.1
  22.3 1.6 %collective-permute-start.1 = (bf16[256,512]{1,0:T(8,128)(2,1)}, bf16[256,512]{1,0:T(8,128)(2,1)S(1)}, u32[]{:S(2)}, u32[]{:S(2)}) collective-permute-start(bf16[256,512]{1,0:T(8,128)(2,1)} %refs_0_.3), channel_id=1, source_target_pairs={{0,2},{1,3},{2,0},{3,1},{4,6},{5,7},{6,4},{7,5},{8,10},{9,11},{10,... | collective-permute-start | bytes 786440 | tf_op jit(solution)/shard_map/ppermute | solution.py:26
  23.9 4.5 %collective-permute-done.7.refs_6_.refs_8_ = bf16[256,512]{1,0:T(8,128)(2,1)S(1)} collective-permute-done((bf16[256,512]{1,0:T(8,128)(2,1)}, bf16[256,512]{1,0:T(8,128)(2,1)S(1)}, u32[]{:S(2)}, u32[]{:S(2)}) %collective-permute-start.7) | collective-permute-done | bytes 262176 | tf_op jit(solution)/shard_map/ppermute | solution.py:26
  28.4 2.4 %collective-permute-done.8.refs_7_.refs_9_ = bf16[256,512]{1,0:T(8,128)(2,1)S(1)} collective-permute-done((bf16[256,512]{1,0:T(8,128)(2,1)}, bf16[256,512]{1,0:T(8,128)(2,1)S(1)}, u32[]{:S(2)}, u32[]{:S(2)}) %collective-permute-start.8) | collective-permute-done | bytes 262176 | tf_op jit(solution)/shard_map/ppermute | solution.py:26
  30.8 0.9 copy-done.3
  32.2 0.6 collective-permute-start.11
  33.3 2.6 %collective-permute-start.13 = (bf16[256,512]{1,0:T(8,128)(2,1)S(1)}, bf16[256,512]{1,0:T(8,128)(2,1)S(1)}, u32[]{:S(2)}, u32[]{:S(2)}) collective-permute-start(bf16[256,512]{1,0:T(8,128)(2,1)S(1)} %shard_map.107.refs_2_), channel_id=1, source_target_pairs={{0,12},{4,8},{8,4},{12,0},{16,28},{20,24},{24,20},{28,16},{1,13},{... | collective-permute-start | bytes 786440 | tf_op jit(solution)/shard_map/ppermute | solution.py:26
  36.4 0.8 collective-permute-done.2.refs_3_
  37.2 0.7 shard_map.102.grad.refs_1_
  38.0 2.0 %shard_map.103 = (f32[256,2048]{1,0:T(8,128)S(1)}, f32[256,2048]{1,0:T(8,128)S(1)}, f32[256,128]{1,0:T(8,128)S(1)}) custom-call(s32[3,16]{1,0:T(4,128)S(1)} %bitcast.2, bf16[256,512]{1,0:T(8,128)(2,1)S(1)} %copy-done.5, bf16[256,512]{1,0:T(8,128)(2,1)S(1)} %shard_map.102.grad.refs_1_, bf16[256,512]{1,0:T(8,128)(2,1)S(1)} %copy-done.2, ...), custom_call_target="tpu_custom_call" | custom-call | tf_op jit(solution)/shard_map/pallas_call | solution.py:34
  39.9 0.6 collective-permute-done.11.refs_3_
  40.6 1.4 %collective-permute-done.12.refs_4_ = bf16[256,512]{1,0:T(8,128)(2,1)S(1)} collective-permute-done((bf16[256,512]{1,0:T(8,128)(2,1)S(1)}, bf16[256,512]{1,0:T(8,128)(2,1)S(1)}, u32[]{:S(2)}, u32[]{:S(2)}) %collective-permute-start.12) | collective-permute-done | bytes 262176 | tf_op jit(solution)/shard_map/ppermute | solution.py:26
  42.0 6.6 %collective-permute-done.13.refs_5_ = bf16[256,512]{1,0:T(8,128)(2,1)S(1)} collective-permute-done((bf16[256,512]{1,0:T(8,128)(2,1)S(1)}, bf16[256,512]{1,0:T(8,128)(2,1)S(1)}, u32[]{:S(2)}, u32[]{:S(2)}) %collective-permute-start.13) | collective-permute-done | bytes 262176 | tf_op jit(solution)/shard_map/ppermute | solution.py:26
  48.5 2.6 %collective-permute-done.10.refs_1_ = bf16[256,512]{1,0:T(8,128)(2,1)S(1)} collective-permute-done((bf16[256,512]{1,0:T(8,128)(2,1)S(1)}, bf16[256,512]{1,0:T(8,128)(2,1)S(1)}, u32[]{:S(2)}, u32[]{:S(2)}) %collective-permute-start.10) | collective-permute-done | bytes 262176 | tf_op jit(solution)/shard_map/ppermute | solution.py:26
  51.1 2.7 %shard_map.108 = (f32[256,512]{1,0:T(8,128)S(1)}, bf16[256,512]{1,0:T(8,128)(2,1)S(1)}, f32[32,256]{1,0:T(8,128)S(1)}, f32[256,128]{1,0:T(8,128)S(1)}, bf16[256,...) custom-call(bf16[256,512]{1,0:T(8,128)(2,1)S(1)} %copy-done.5, ...), custom_call_target="tpu_custom_call" | custom-call | tf_op jit(solution)/shard_map/pallas_call | solution.py:34
  53.8 1.6 %collective-permute-start.26 = (bf16[256,512]{1,0:T(8,128)(2,1)S(1)}, bf16[256,512]{1,0:T(8,128)(2,1)S(1)}, u32[]{:S(2)}, u32[]{:S(2)}) collective-permute-start(bf16[256,512]{1,0:T(8,128)(2,1)S(1)} %get-tuple-element.65), channel_id=1, source_target_pairs={{0,4},{4,0},{8,12},{12,8},{16,20},{20,16},{24,28},{28,24},{1,5},{5... | collective-permute-start | bytes 786440 | tf_op jit(solution)/shard_map/ppermute | solution.py:26
  55.4 0.5 collective-permute-start.17
  55.9 7.0 %collective-permute-done.26 = bf16[256,512]{1,0:T(8,128)(2,1)S(1)} collective-permute-done((bf16[256,512]{1,0:T(8,128)(2,1)S(1)}, bf16[256,512]{1,0:T(8,128)(2,1)S(1)}, u32[]{:S(2)}, u32[]{:S(2)}) %collective-permute-start.26) | collective-permute-done | bytes 262176 | tf_op jit(solution)/shard_map/ppermute | solution.py:26
  63.3 1.9 %collective-permute-start.18 = (bf16[256,512]{1,0:T(8,128)(2,1)S(1)}, bf16[256,512]{1,0:T(8,128)(2,1)S(1)}, u32[]{:S(2)}, u32[]{:S(2)}) collective-permute-start(bf16[256,512]{1,0:T(8,128)(2,1)S(1)} %copy-done.5), channel_id=1, source_target_pairs={{0,8},{4,12},{8,0},{12,4},{16,24},{20,28},{24,16},{28,20},{1,9},{5... | collective-permute-start | bytes 786440 | tf_op jit(solution)/shard_map/ppermute | solution.py:26
  65.1 1.4 %collective-permute-start.19 = (bf16[256,512]{1,0:T(8,128)(2,1)S(1)}, bf16[256,512]{1,0:T(8,128)(2,1)S(1)}, u32[]{:S(2)}, u32[]{:S(2)}) collective-permute-start(bf16[256,512]{1,0:T(8,128)(2,1)S(1)} %copy-done.5), channel_id=1, source_target_pairs={{0,16},{4,20},{8,24},{12,28},{16,0},{20,4},{24,8},{28,12},{1,17},{... | collective-permute-start | bytes 786440 | tf_op jit(solution)/shard_map/ppermute | solution.py:26
  66.6 1.5 %collective-permute-start.20 = (bf16[256,512]{1,0:T(8,128)(2,1)S(1)}, bf16[256,512]{1,0:T(8,128)(2,1)S(1)}, u32[]{:S(2)}, u32[]{:S(2)}) collective-permute-start(bf16[256,512]{1,0:T(8,128)(2,1)S(1)} %shard_map.102.grad.refs_1_), channel_id=1, source_target_pairs={{0,4},{4,0},{8,12},{12,8},{16,20},{20,16},{24,28},{28,24},{1,5},{5... | collective-permute-start | bytes 786440 | tf_op jit(solution)/shard_map/ppermute | solution.py:26
  68.3 1.5 %collective-permute-start.21 = (bf16[256,512]{1,0:T(8,128)(2,1)S(1)}, bf16[256,512]{1,0:T(8,128)(2,1)S(1)}, u32[]{:S(2)}, u32[]{:S(2)}) collective-permute-start(bf16[256,512]{1,0:T(8,128)(2,1)S(1)} %shard_map.102.grad.refs_1_), channel_id=1, source_target_pairs={{0,8},{4,12},{8,0},{12,4},{16,24},{20,28},{24,16},{28,20},{1,9},{5... | collective-permute-start | bytes 786440 | tf_op jit(solution)/shard_map/ppermute | solution.py:26
  69.8 8.1 %collective-permute-done.27 = bf16[256,512]{1,0:T(8,128)(2,1)S(1)} collective-permute-done((bf16[256,512]{1,0:T(8,128)(2,1)S(1)}, bf16[256,512]{1,0:T(8,128)(2,1)S(1)}, u32[]{:S(2)}, u32[]{:S(2)}) %collective-permute-start.27) | collective-permute-done | bytes 262176 | tf_op jit(solution)/shard_map/ppermute | solution.py:26
  77.9 0.7 collective-permute-start.22
  78.7 4.0 %collective-permute-done.18.refs_1_ = bf16[256,512]{1,0:T(8,128)(2,1)S(1)} collective-permute-done((bf16[256,512]{1,0:T(8,128)(2,1)S(1)}, bf16[256,512]{1,0:T(8,128)(2,1)S(1)}, u32[]{:S(2)}, u32[]{:S(2)}) %collective-permute-start.18) | collective-permute-done | bytes 262176 | tf_op jit(solution)/shard_map/ppermute | solution.py:26
  82.7 5.7 %collective-permute-start.28 = (bf16[256,512]{1,0:T(8,128)(2,1)S(1)}, bf16[256,512]{1,0:T(8,128)(2,1)S(1)}, u32[]{:S(2)}, u32[]{:S(2)}) collective-permute-start(bf16[256,512]{1,0:T(8,128)(2,1)S(1)} %fusion.1), channel_id=1, source_target_pairs={{0,24},{4,28},{8,16},{12,20},{16,8},{20,12},{24,0},{28,4},{1,25},{... | collective-permute-start | bytes 786440 | tf_op jit(solution)/shard_map/ppermute | solution.py:26
  88.4 1.5 %collective-permute-start.23 = (f32[32,256]{1,0:T(8,128)S(1)}, f32[32,256]{1,0:T(8,128)S(1)}, u32[]{:S(2)}, u32[]{:S(2)}) collective-permute-start(f32[32,256]{1,0:T(8,128)S(1)} %get-tuple-element.59.refs_2_), channel_id=1, source_target_pairs={{0,4},{4,0},{8,12},{12,8},{16,20},{20,16},{24,28},{28,24},{1,5},{5... | collective-permute-start | bytes 98312 | tf_op jit(solution)/shard_map/ppermute | solution.py:26
  90.6 2.5 %shard_map.111 = (f32[256,512]{1,0:T(8,128)S(1)}, f32[256,512]{1,0:T(8,128)S(1)}) custom-call(s32[3,16]{1,0:T(4,128)S(1)} %bitcast.3, bf16[256,512]{1,0:T(8,128)(2,1)S(1)} %copy-done.2, bf16[256,512]{1,0:T(8,128)(2,1)S(1)} %copy-done.4, bf16[256,512]{1,0:T(8,128)(2,1)S(1)} %copy-done.5, bf16[256,512]{1,0:T(8,128)(2,1)S(1)} %shard_map.102.grad.refs_1_, ...), custom_call_target="tpu_custom_call" | custom-call | tf_op jit(solution)/shard_map/pallas_call | solution.py:34
  93.1 2.8 %shard_map.109 = (bf16[256,512]{1,0:T(8,128)(2,1)S(1)}, bf16[256,512]{1,0:T(8,128)(2,1)}) custom-call(s32[3,16]{1,0:T(4,128)S(1)} %bitcast.4, f32[256,2048]{1,0:T(8,128)S(1)} %get-tuple-element.36.exponents, f32[256,2048]{1,0:T(8,128)S(1)} %get-tuple-element.37.probs, f32[256,128]{1,0:T(8,128)S(1)} %get-tuple-element.47.rest, ...), custom_call_target="tpu_custom_call" | custom-call | tf_op jit(solution)/shard_map/pallas_call | solution.py:34
  96.0 0.7 shard_map.110
  96.7 1.1 collective-permute-done.22.refs_5_
  97.8 1.8 %collective-permute-start.14 = (bf16[256,512]{1,0:T(8,128)(2,1)S(1)}, bf16[256,512]{1,0:T(8,128)(2,1)S(1)}, u32[]{:S(2)}, u32[]{:S(2)}) collective-permute-start(bf16[256,512]{1,0:T(8,128)(2,1)S(1)} %get-tuple-element.54), channel_id=1, source_target_pairs={{0,1},{1,0},{2,3},{3,2},{4,5},{5,4},{6,7},{7,6},{8,9},{9,8},{10,11... | collective-permute-start | bytes 786440 | tf_op jit(solution)/shard_map/ppermute | solution.py:26
  99.6 1.3 %collective-permute-done.25.refs_8_ = f32[32,256]{1,0:T(8,128)S(1)} collective-permute-done((f32[32,256]{1,0:T(8,128)S(1)}, f32[32,256]{1,0:T(8,128)S(1)}, u32[]{:S(2)}, u32[]{:S(2)}) %collective-permute-start.25) | collective-permute-done | bytes 32800 | tf_op jit(solution)/shard_map/ppermute | solution.py:26
  100.9 5.3 %shard_map.112 = (f32[256,512]{1,0:T(8,128)S(1)}, f32[256,512]{1,0:T(8,128)S(1)}) custom-call(s32[3,16]{1,0:T(4,128)S(1)} %bitcast.5, bf16[256,512]{1,0:T(8,128)(2,1)S(1)} %copy-done.2, bf16[256,512]{1,0:T(8,128)(2,1)S(1)} %copy-done.4, bf16[256,512]{1,0:T(8,128)(2,1)S(1)} %collective-permute-done.17.refs_0_, ...), custom_call_target="tpu_custom_call" | custom-call | tf_op jit(solution)/shard_map/pallas_call | solution.py:34
  106.4 1.5 %collective-permute-start.29 = (bf16[256,512]{1,0:T(8,128)(2,1)S(1)}, bf16[256,512]{1,0:T(8,128)(2,1)S(1)}, u32[]{:S(2)}, u32[]{:S(2)}) collective-permute-start(bf16[256,512]{1,0:T(8,128)(2,1)S(1)} %add_convert_fusion.kept), channel_id=1, source_target_pairs={{0,4},{4,0},{8,12},{12,8},{16,20},{20,16},{24,28},{28,24},{1,5},{5... | collective-permute-start | bytes 786440 | tf_op jit(solution)/shard_map/ppermute | solution.py:26
  107.9 0.8 collective-permute-done.15
  108.7 0.9 add_convert_fusion.1
  109.6 3.8 %collective-permute-done.29.got = bf16[256,512]{1,0:T(8,128)(2,1)S(1)} collective-permute-done((bf16[256,512]{1,0:T(8,128)(2,1)S(1)}, bf16[256,512]{1,0:T(8,128)(2,1)S(1)}, u32[]{:S(2)}, u32[]{:S(2)}) %collective-permute-start.29) | collective-permute-done | bytes 262176 | tf_op jit(solution)/shard_map/ppermute | solution.py:26
  113.4 1.1 shard_map.113
  (46 shorter events, 4.3 us)
Async XLA Ops:
  0.6 10.1 %collective-permute-start.3 = (bf16[256,512]{1,0:T(8,128)(2,1)}, bf16[256,512]{1,0:T(8,128)(2,1)S(1)}, u32[]{:S(2)}, u32[]{:S(2)}) collective-permute-start(bf16[256,512]{1,0:T(8,128)(2,1)} %key.3), channel_id=1, source_target_pairs={{0,4},{4,0},{8,12},{12,8},{16,20},{20,16},{24,28},{28,24},{1,5},{5... | collective-permute-start | bytes 786440 | tf_op jit(solution)/shard_map/ppermute | solution.py:26
  3.7 15.4 %collective-permute-start.4 = (bf16[256,512]{1,0:T(8,128)(2,1)}, bf16[256,512]{1,0:T(8,128)(2,1)S(1)}, u32[]{:S(2)}, u32[]{:S(2)}) collective-permute-start(bf16[256,512]{1,0:T(8,128)(2,1)} %key.3), channel_id=1, source_target_pairs={{0,8},{4,12},{8,0},{12,4},{16,24},{20,28},{24,16},{28,20},{1,9},{5... | collective-permute-start | bytes 786440 | tf_op jit(solution)/shard_map/ppermute | solution.py:26
  5.3 15.4 %collective-permute-start.5 = (bf16[256,512]{1,0:T(8,128)(2,1)}, bf16[256,512]{1,0:T(8,128)(2,1)S(1)}, u32[]{:S(2)}, u32[]{:S(2)}) collective-permute-start(bf16[256,512]{1,0:T(8,128)(2,1)} %key.3), channel_id=1, source_target_pairs={{0,16},{4,20},{8,24},{12,28},{16,0},{20,4},{24,8},{28,12},{1,17},{... | collective-permute-start | bytes 786440 | tf_op jit(solution)/shard_map/ppermute | solution.py:26
  7.9 14.4 %collective-permute-start.6 = (bf16[256,512]{1,0:T(8,128)(2,1)}, bf16[256,512]{1,0:T(8,128)(2,1)S(1)}, u32[]{:S(2)}, u32[]{:S(2)}) collective-permute-start(bf16[256,512]{1,0:T(8,128)(2,1)} %value.3), channel_id=1, source_target_pairs={{0,4},{4,0},{8,12},{12,8},{16,20},{20,16},{24,28},{28,24},{1,5},{5... | collective-permute-start | bytes 786440 | tf_op jit(solution)/shard_map/ppermute | solution.py:26
  8.4 20.0 %collective-permute-start.7 = (bf16[256,512]{1,0:T(8,128)(2,1)}, bf16[256,512]{1,0:T(8,128)(2,1)S(1)}, u32[]{:S(2)}, u32[]{:S(2)}) collective-permute-start(bf16[256,512]{1,0:T(8,128)(2,1)} %value.3), channel_id=1, source_target_pairs={{0,8},{4,12},{8,0},{12,4},{16,24},{20,28},{24,16},{28,20},{1,9},{5... | collective-permute-start | bytes 786440 | tf_op jit(solution)/shard_map/ppermute | solution.py:26
  8.8 0.7 copy-start.8
  10.8 20.1 %collective-permute-start.8 = (bf16[256,512]{1,0:T(8,128)(2,1)}, bf16[256,512]{1,0:T(8,128)(2,1)S(1)}, u32[]{:S(2)}, u32[]{:S(2)}) collective-permute-start(bf16[256,512]{1,0:T(8,128)(2,1)} %value.3), channel_id=1, source_target_pairs={{0,16},{4,20},{8,24},{12,28},{16,0},{20,4},{24,8},{28,12},{1,17},{... | collective-permute-start | bytes 786440 | tf_op jit(solution)/shard_map/ppermute | solution.py:26
  20.7 1.0 copy-start.1
  21.7 15.5 %copy-start = (bf16[512,2048]{1,0:T(8,128)(2,1)S(1)}, bf16[512,2048]{1,0:T(8,128)(2,1)}, u32[]{:S(2)}) copy-start(bf16[512,2048]{1,0:T(8,128)(2,1)} %weight_ref.3) | copy-start | bytes 6291460
  22.1 10.7 %collective-permute-start.9 = (bf16[256,512]{1,0:T(8,128)(2,1)S(1)}, bf16[256,512]{1,0:T(8,128)(2,1)S(1)}, u32[]{:S(2)}, u32[]{:S(2)}) collective-permute-start(bf16[256,512]{1,0:T(8,128)(2,1)S(1)} %shard_map.105.have), channel_id=1, source_target_pairs={{0,4},{4,0},{8,12},{12,8},{16,20},{20,16},{24,28},{28,24},{1,5},{5... | collective-permute-start | bytes 786440 | tf_op jit(solution)/shard_map/ppermute | solution.py:26
  22.2 11.2 %collective-permute-start = (bf16[256,512]{1,0:T(8,128)(2,1)}, bf16[256,512]{1,0:T(8,128)(2,1)S(1)}, u32[]{:S(2)}, u32[]{:S(2)}) collective-permute-start(bf16[256,512]{1,0:T(8,128)(2,1)} %refs_0_.3), channel_id=1, source_target_pairs={{0,1},{1,0},{2,3},{3,2},{4,5},{5,4},{6,7},{7,6},{8,9},{9,8},{10,11... | collective-permute-start | bytes 786440 | tf_op jit(solution)/shard_map/ppermute | solution.py:26
  22.3 13.7 %collective-permute-start.1 = (bf16[256,512]{1,0:T(8,128)(2,1)}, bf16[256,512]{1,0:T(8,128)(2,1)S(1)}, u32[]{:S(2)}, u32[]{:S(2)}) collective-permute-start(bf16[256,512]{1,0:T(8,128)(2,1)} %refs_0_.3), channel_id=1, source_target_pairs={{0,2},{1,3},{2,0},{3,1},{4,6},{5,7},{6,4},{7,5},{8,10},{9,11},{10,... | collective-permute-start | bytes 786440 | tf_op jit(solution)/shard_map/ppermute | solution.py:26
  28.4 8.8 %collective-permute-start.2 = (bf16[256,512]{1,0:T(8,128)(2,1)}, bf16[256,512]{1,0:T(8,128)(2,1)S(1)}, u32[]{:S(2)}, u32[]{:S(2)}) collective-permute-start(bf16[256,512]{1,0:T(8,128)(2,1)} %refs_0_.3), channel_id=1, source_target_pairs={{0,3},{1,2},{2,1},{3,0},{4,7},{5,6},{6,5},{7,4},{8,11},{9,10},{10,... | collective-permute-start | bytes 786440 | tf_op jit(solution)/shard_map/ppermute | solution.py:26
  30.8 1.0 copy-start.3
  31.8 5.4 %copy-start.6 = (bf16[256,512]{1,0:T(8,128)(2,1)S(1)}, bf16[256,512]{1,0:T(8,128)(2,1)}, u32[]{:S(2)}) copy-start(bf16[256,512]{1,0:T(8,128)(2,1)} %refs_0_.3) | copy-start | bytes 786436
  32.2 8.3 %collective-permute-start.11 = (bf16[256,512]{1,0:T(8,128)(2,1)S(1)}, bf16[256,512]{1,0:T(8,128)(2,1)S(1)}, u32[]{:S(2)}, u32[]{:S(2)}) collective-permute-start(bf16[256,512]{1,0:T(8,128)(2,1)S(1)} %shard_map.107.refs_2_), channel_id=1, source_target_pairs={{0,4},{4,0},{8,12},{12,8},{16,20},{20,16},{24,28},{28,24},{1,5},{5... | collective-permute-start | bytes 786440 | tf_op jit(solution)/shard_map/ppermute | solution.py:26
  32.8 9.2 %collective-permute-start.12 = (bf16[256,512]{1,0:T(8,128)(2,1)S(1)}, bf16[256,512]{1,0:T(8,128)(2,1)S(1)}, u32[]{:S(2)}, u32[]{:S(2)}) collective-permute-start(bf16[256,512]{1,0:T(8,128)(2,1)S(1)} %shard_map.107.refs_2_), channel_id=1, source_target_pairs={{0,8},{4,12},{8,0},{12,4},{16,24},{20,28},{24,16},{28,20},{1,9},{5... | collective-permute-start | bytes 786440 | tf_op jit(solution)/shard_map/ppermute | solution.py:26
  33.2 4.7 %copy-start.2 = (bf16[256,512]{1,0:T(8,128)(2,1)S(1)}, bf16[256,512]{1,0:T(8,128)(2,1)}, u32[]{:S(2)}) copy-start(bf16[256,512]{1,0:T(8,128)(2,1)} %key.3) | copy-start | bytes 786436
  33.2 4.7 %copy-start.4 = (bf16[256,512]{1,0:T(8,128)(2,1)S(1)}, bf16[256,512]{1,0:T(8,128)(2,1)}, u32[]{:S(2)}) copy-start(bf16[256,512]{1,0:T(8,128)(2,1)} %value.3) | copy-start | bytes 786436
  33.2 4.7 %copy-start.5 = (bf16[256,512]{1,0:T(8,128)(2,1)S(1)}, bf16[256,512]{1,0:T(8,128)(2,1)}, u32[]{:S(2)}) copy-start(bf16[256,512]{1,0:T(8,128)(2,1)} %refs_0_.5) | copy-start | bytes 786436
  33.2 4.7 %copy-start.7 = (s32[16,3]{0,1:T(4,128)S(1)}, s32[16,3]{0,1:T(4,128)}, u32[]{:S(2)}) copy-start(s32[16,3]{0,1:T(4,128)} %param.12) | copy-start | bytes 580
  33.3 15.2 %collective-permute-start.13 = (bf16[256,512]{1,0:T(8,128)(2,1)S(1)}, bf16[256,512]{1,0:T(8,128)(2,1)S(1)}, u32[]{:S(2)}, u32[]{:S(2)}) collective-permute-start(bf16[256,512]{1,0:T(8,128)(2,1)S(1)} %shard_map.107.refs_2_), channel_id=1, source_target_pairs={{0,12},{4,8},{8,4},{12,0},{16,28},{20,24},{24,20},{28,16},{1,13},{... | collective-permute-start | bytes 786440 | tf_op jit(solution)/shard_map/ppermute | solution.py:26
  36.0 15.2 %collective-permute-start.10 = (bf16[256,512]{1,0:T(8,128)(2,1)S(1)}, bf16[256,512]{1,0:T(8,128)(2,1)S(1)}, u32[]{:S(2)}, u32[]{:S(2)}) collective-permute-start(bf16[256,512]{1,0:T(8,128)(2,1)S(1)} %shard_map.106.refs_0_), channel_id=1, source_target_pairs={{0,8},{4,12},{8,0},{12,4},{16,24},{20,28},{24,16},{28,20},{1,9},{5... | collective-permute-start | bytes 786440 | tf_op jit(solution)/shard_map/ppermute | solution.py:26
  53.8 9.1 %collective-permute-start.26 = (bf16[256,512]{1,0:T(8,128)(2,1)S(1)}, bf16[256,512]{1,0:T(8,128)(2,1)S(1)}, u32[]{:S(2)}, u32[]{:S(2)}) collective-permute-start(bf16[256,512]{1,0:T(8,128)(2,1)S(1)} %get-tuple-element.65), channel_id=1, source_target_pairs={{0,4},{4,0},{8,12},{12,8},{16,20},{20,16},{24,28},{28,24},{1,5},{5... | collective-permute-start | bytes 786440 | tf_op jit(solution)/shard_map/ppermute | solution.py:26
  55.4 12.9 %collective-permute-start.17 = (bf16[256,512]{1,0:T(8,128)(2,1)S(1)}, bf16[256,512]{1,0:T(8,128)(2,1)S(1)}, u32[]{:S(2)}, u32[]{:S(2)}) collective-permute-start(bf16[256,512]{1,0:T(8,128)(2,1)S(1)} %copy-done.5), channel_id=1, source_target_pairs={{0,4},{4,0},{8,12},{12,8},{16,20},{20,16},{24,28},{28,24},{1,5},{5... | collective-permute-start | bytes 786440 | tf_op jit(solution)/shard_map/ppermute | solution.py:26
  63.1 14.9 %collective-permute-start.27 = (bf16[256,512]{1,0:T(8,128)(2,1)S(1)}, bf16[256,512]{1,0:T(8,128)(2,1)S(1)}, u32[]{:S(2)}, u32[]{:S(2)}) collective-permute-start(bf16[256,512]{1,0:T(8,128)(2,1)S(1)} %fusion), channel_id=1, source_target_pairs={{0,8},{4,12},{8,0},{12,4},{16,24},{20,28},{24,16},{28,20},{1,9},{5... | collective-permute-start | bytes 786440 | tf_op jit(solution)/shard_map/ppermute | solution.py:26
  63.3 19.5 %collective-permute-start.18 = (bf16[256,512]{1,0:T(8,128)(2,1)S(1)}, bf16[256,512]{1,0:T(8,128)(2,1)S(1)}, u32[]{:S(2)}, u32[]{:S(2)}) collective-permute-start(bf16[256,512]{1,0:T(8,128)(2,1)S(1)} %copy-done.5), channel_id=1, source_target_pairs={{0,8},{4,12},{8,0},{12,4},{16,24},{20,28},{24,16},{28,20},{1,9},{5... | collective-permute-start | bytes 786440 | tf_op jit(solution)/shard_map/ppermute | solution.py:26
  65.1 23.2 %collective-permute-start.19 = (bf16[256,512]{1,0:T(8,128)(2,1)S(1)}, bf16[256,512]{1,0:T(8,128)(2,1)S(1)}, u32[]{:S(2)}, u32[]{:S(2)}) collective-permute-start(bf16[256,512]{1,0:T(8,128)(2,1)S(1)} %copy-done.5), channel_id=1, source_target_pairs={{0,16},{4,20},{8,24},{12,28},{16,0},{20,4},{24,8},{28,12},{1,17},{... | collective-permute-start | bytes 786440 | tf_op jit(solution)/shard_map/ppermute | solution.py:26
  66.6 23.3 %collective-permute-start.20 = (bf16[256,512]{1,0:T(8,128)(2,1)S(1)}, bf16[256,512]{1,0:T(8,128)(2,1)S(1)}, u32[]{:S(2)}, u32[]{:S(2)}) collective-permute-start(bf16[256,512]{1,0:T(8,128)(2,1)S(1)} %shard_map.102.grad.refs_1_), channel_id=1, source_target_pairs={{0,4},{4,0},{8,12},{12,8},{16,20},{20,16},{24,28},{28,24},{1,5},{5... | collective-permute-start | bytes 786440 | tf_op jit(solution)/shard_map/ppermute | solution.py:26
  68.3 21.9 %collective-permute-start.21 = (bf16[256,512]{1,0:T(8,128)(2,1)S(1)}, bf16[256,512]{1,0:T(8,128)(2,1)S(1)}, u32[]{:S(2)}, u32[]{:S(2)}) collective-permute-start(bf16[256,512]{1,0:T(8,128)(2,1)S(1)} %shard_map.102.grad.refs_1_), channel_id=1, source_target_pairs={{0,8},{4,12},{8,0},{12,4},{16,24},{20,28},{24,16},{28,20},{1,9},{5... | collective-permute-start | bytes 786440 | tf_op jit(solution)/shard_map/ppermute | solution.py:26
  77.9 19.8 %collective-permute-start.22 = (bf16[256,512]{1,0:T(8,128)(2,1)S(1)}, bf16[256,512]{1,0:T(8,128)(2,1)S(1)}, u32[]{:S(2)}, u32[]{:S(2)}) collective-permute-start(bf16[256,512]{1,0:T(8,128)(2,1)S(1)} %shard_map.102.grad.refs_1_), channel_id=1, source_target_pairs={{0,16},{4,20},{8,24},{12,28},{16,0},{20,4},{24,8},{28,12},{1,17},{... | collective-permute-start | bytes 786440 | tf_op jit(solution)/shard_map/ppermute | solution.py:26
  82.7 23.5 %collective-permute-start.28 = (bf16[256,512]{1,0:T(8,128)(2,1)S(1)}, bf16[256,512]{1,0:T(8,128)(2,1)S(1)}, u32[]{:S(2)}, u32[]{:S(2)}) collective-permute-start(bf16[256,512]{1,0:T(8,128)(2,1)S(1)} %fusion.1), channel_id=1, source_target_pairs={{0,24},{4,28},{8,16},{12,20},{16,8},{20,12},{24,0},{28,4},{1,25},{... | collective-permute-start | bytes 786440 | tf_op jit(solution)/shard_map/ppermute | solution.py:26
  88.4 9.3 %collective-permute-start.23 = (f32[32,256]{1,0:T(8,128)S(1)}, f32[32,256]{1,0:T(8,128)S(1)}, u32[]{:S(2)}, u32[]{:S(2)}) collective-permute-start(f32[32,256]{1,0:T(8,128)S(1)} %get-tuple-element.59.refs_2_), channel_id=1, source_target_pairs={{0,4},{4,0},{8,12},{12,8},{16,20},{20,16},{24,28},{28,24},{1,5},{5... | collective-permute-start | bytes 98312 | tf_op jit(solution)/shard_map/ppermute | solution.py:26
  89.9 7.8 %collective-permute-start.24 = (f32[32,256]{1,0:T(8,128)S(1)}, f32[32,256]{1,0:T(8,128)S(1)}, u32[]{:S(2)}, u32[]{:S(2)}) collective-permute-start(f32[32,256]{1,0:T(8,128)S(1)} %get-tuple-element.59.refs_2_), channel_id=1, source_target_pairs={{0,8},{4,12},{8,0},{12,4},{16,24},{20,28},{24,16},{28,20},{1,9},{5... | collective-permute-start | bytes 98312 | tf_op jit(solution)/shard_map/ppermute | solution.py:26
  90.2 10.7 %collective-permute-start.25 = (f32[32,256]{1,0:T(8,128)S(1)}, f32[32,256]{1,0:T(8,128)S(1)}, u32[]{:S(2)}, u32[]{:S(2)}) collective-permute-start(f32[32,256]{1,0:T(8,128)S(1)} %get-tuple-element.59.refs_2_), channel_id=1, source_target_pairs={{0,16},{4,20},{8,24},{12,28},{16,0},{20,4},{24,8},{28,12},{1,17},{... | collective-permute-start | bytes 98312 | tf_op jit(solution)/shard_map/ppermute | solution.py:26
  97.7 10.2 %collective-permute-start.16 = (bf16[256,512]{1,0:T(8,128)(2,1)S(1)}, bf16[256,512]{1,0:T(8,128)(2,1)S(1)}, u32[]{:S(2)}, u32[]{:S(2)}) collective-permute-start(bf16[256,512]{1,0:T(8,128)(2,1)S(1)} %get-tuple-element.56), channel_id=1, source_target_pairs={{0,3},{1,2},{2,1},{3,0},{4,7},{5,6},{6,5},{7,4},{8,11},{9,10},{10,... | collective-permute-start | bytes 786440 | tf_op jit(solution)/shard_map/ppermute | solution.py:26
  97.7 11.0 %collective-permute-start.15 = (bf16[256,512]{1,0:T(8,128)(2,1)S(1)}, bf16[256,512]{1,0:T(8,128)(2,1)S(1)}, u32[]{:S(2)}, u32[]{:S(2)}) collective-permute-start(bf16[256,512]{1,0:T(8,128)(2,1)S(1)} %get-tuple-element.55), channel_id=1, source_target_pairs={{0,2},{1,3},{2,0},{3,1},{4,6},{5,7},{6,4},{7,5},{8,10},{9,11},{10,... | collective-permute-start | bytes 786440 | tf_op jit(solution)/shard_map/ppermute | solution.py:26
  97.8 11.0 %collective-permute-start.14 = (bf16[256,512]{1,0:T(8,128)(2,1)S(1)}, bf16[256,512]{1,0:T(8,128)(2,1)S(1)}, u32[]{:S(2)}, u32[]{:S(2)}) collective-permute-start(bf16[256,512]{1,0:T(8,128)(2,1)S(1)} %get-tuple-element.54), channel_id=1, source_target_pairs={{0,1},{1,0},{2,3},{3,2},{4,5},{5,4},{6,7},{7,6},{8,9},{9,8},{10,11... | collective-permute-start | bytes 786440 | tf_op jit(solution)/shard_map/ppermute | solution.py:26
  106.4 7.0 %collective-permute-start.29 = (bf16[256,512]{1,0:T(8,128)(2,1)S(1)}, bf16[256,512]{1,0:T(8,128)(2,1)S(1)}, u32[]{:S(2)}, u32[]{:S(2)}) collective-permute-start(bf16[256,512]{1,0:T(8,128)(2,1)S(1)} %add_convert_fusion.kept), channel_id=1, source_target_pairs={{0,4},{4,0},{8,12},{12,8},{16,20},{20,16},{24,28},{28,24},{1,5},{5... | collective-permute-start | bytes 786440 | tf_op jit(solution)/shard_map/ppermute | solution.py:26
